TPU v7x, 512 devices: a whole 4x8x8 slice. The times are simulated.
512 devices in a mesh: dp: 16 (over y, core), seq: 32 (over z, x).
Axes of the slice: x: 4, y: 8, z: 8, core: 2. Of those that a mesh axis runs over, the one named last changes fastest.
Arguments:
- hidden: bfloat16 [65536, 2048], P(('dp', 'seq')), may hold values from -6 to 6
- queries: bfloat16 [65536, 2048], P(('dp', 'seq')), may hold values from -360 to 360
- values: bfloat16 [65536, 512], P(('dp', 'seq')), may hold values from -6 to 6
- row_target: int32 [65536], P(('dp', 'seq')), may hold values from 0 to 4095, as said below
- key_weight: bfloat16 [2048, 512], P(('dp', 'seq')), may hold values from -0.125 to 0.125
- dialogue_lengths: int32 [16, 64], P('dp'), may hold values from 1 to 256, 4096 in all within a row
- teacher_pick: int32 [65536, 128], P(('dp', 'seq')), may hold values from 0 to 65279
- teacher_prob: float32 [65536, 128], P(('dp', 'seq')), may hold values from 0.02 to 1
Outputs:
- attn_out: bfloat16 [65536, 2048], P(('dp', 'seq'))
- token_loss: float32 [65536], P(('dp', 'seq'))
- weight_grad: float32 [2048, 512], P(('dp', 'seq'))
Inputs may be any that keep to these rules, and one draw needn't show every extreme that they name: Within each pack, row_target holds every position 0 to 4095 once. Of the 128 rows of one device, at most 6 have targets in one block of 128 positions (target // 128 names the block), and in every draw some device sends exactly 6 to some block.
All inputs are finite; a program needn't handle non-finite values.
Results may differ from a plain program's by a relative error of at most 0.012.
The roundings to bfloat16 on the way count: a program that leaves them out, or rounds other values in their place, can miss the bound.
Values may be sent and summed in bfloat16 or wider, within the bound.
No kernel may reach another device: no remote copies, remote signals or barrier semaphores. Data moves between devices by JAX's collectives and lax.ppermute only.
A program may use at most 64 MiB of HBM per device.

v0:
```python
import functools

import jax
import jax.numpy as jnp
import numpy as np
from jax import lax
from jax.experimental import pallas as pl
from jax.experimental.pallas import tpu as pltpu
from jax.sharding import Mesh
from jax.sharding import PartitionSpec as P


HEAD_DIM = 128
SPAN = 2
SLOTS = 6

negative = -1e30
rope_base = 500000.0

GRANT = pltpu.CompilerParams(vmem_limit_bytes=24 << 20)

ACROSS = ("xh", "xl")
SEQ = ("z",) + ACROSS
EVERY = ("y", "core") + SEQ


def exchange(pieces, axes):
    return lax.all_to_all(pieces, axes, split_axis=0, concat_axis=0, tiled=True)


def seq_shift(shard, by):
    devices = lax.axis_size(SEQ)
    pairs = [(i, i + by) for i in range(devices) if 0 <= i + by < devices]
    return lax.ppermute(shard, SEQ, pairs)


def line_shift(shard, by):
    devices = lax.axis_size("y")
    return lax.ppermute(shard, "y", [(i, (i + by) % devices) for i in range(devices)])


def core_swap(shard):
    return lax.ppermute(shard, "core", [(0, 1), (1, 0)])


def turn_angles(positions):
    halfway = HEAD_DIM // 2
    frequency = rope_base ** (-2.0 * jnp.arange(halfway, dtype=jnp.float32) / HEAD_DIM)
    angle = positions.astype(jnp.float32)[:, None] * frequency[None, :]
    return jnp.cos(angle)[:, None, :], jnp.sin(angle)[:, None, :]


def rotate(matrix, cosine, sine):
    count = matrix.shape[0]
    halfway = HEAD_DIM // 2
    split = matrix.reshape(count, -1, HEAD_DIM)
    first_half = split[..., :halfway]
    second_half = split[..., halfway:]
    joined = jnp.concatenate(
        [first_half * cosine - second_half * sine, second_half * cosine + first_half * sine],
        axis=-1,
    )
    return joined.reshape(count, -1)


def dialogue_starts(lengths, positions):
    ending = jnp.cumsum(lengths)
    picked = jnp.where(ending[None, :] <= positions[:, None], lengths[None, :], 0)
    return jnp.sum(picked, axis=1)


def pack_kernel(target_ref, hidden_ref, queries_ref, values_ref, out_ref):
    bf16, f32 = jnp.bfloat16, jnp.float32
    rows = hidden_ref.shape[0]
    parcels = out_ref.shape[0]
    main = out_ref.shape[1] // HEAD_DIM - 1
    third = main // 3
    refs = (hidden_ref, queries_ref, values_ref)
    tiles = [ref[:, i * HEAD_DIM : (i + 1) * HEAD_DIM] for ref in refs for i in range(ref.shape[1] // HEAD_DIM)]
    target = target_ref[...]
    block = target // rows
    offset = (target - block * rows - rows).astype(f32)
    across = jnp.broadcast_to(block.astype(f32), (rows, rows))
    down = across.T
    first = lax.broadcasted_iota(jnp.int32, (rows, rows), 0)
    second = lax.broadcasted_iota(jnp.int32, (rows, rows), 1)
    rank = jnp.sum(jnp.where((across == down) & (first < second), 1.0, 0.0), axis=0, keepdims=True)
    rank = rank.astype(jnp.int32)
    row = lax.broadcasted_iota(jnp.int32, (parcels, rows), 0)
    place = row % 8
    to_block = block == row // 8
    low = jnp.where(to_block & (place == rank) & (place < SLOTS), 1.0, 0.0)
    lane = lax.broadcasted_iota(jnp.int32, (parcels, HEAD_DIM), 1)
    meta = jnp.zeros((parcels, HEAD_DIM), f32)
    extras = jnp.concatenate(tiles[main:], axis=1)
    for m in range(3):
        high = jnp.where(
            to_block & (place - SLOTS + 2 * m == rank) & (place >= SLOTS), 1.0, 0.0
        )
        place_of = jnp.sum((low + high) * offset, axis=1, keepdims=True) + rows
        meta = jnp.where(lane == m, place_of, meta)
        select = jnp.concatenate([low, high], axis=1).astype(bf16)
        both = jnp.concatenate([jnp.concatenate(tiles[m:main:3], axis=1), extras], axis=0)
        done = jnp.dot(select, both, preferred_element_type=f32).astype(bf16)
        for i in range(third):
            g = 3 * i + m
            out_ref[:, g * HEAD_DIM : (g + 1) * HEAD_DIM] = done[:, i * HEAD_DIM : (i + 1) * HEAD_DIM]
    out_ref[:, main * HEAD_DIM :] = meta.astype(bf16)


def tile_columns(ref, indices):
    return jnp.concatenate([ref[:, g * HEAD_DIM : (g + 1) * HEAD_DIM] for g in indices], axis=1)


def arrivals(got_ref, rows):
    parcels = got_ref.shape[0]
    main = got_ref.shape[1] // HEAD_DIM - 1
    meta = got_ref[:, main * HEAD_DIM :].astype(jnp.float32).T
    token = lax.broadcasted_iota(jnp.int32, (rows, parcels), 0).astype(jnp.float32)
    low = lax.broadcasted_iota(jnp.int32, (rows, parcels), 1) % 8 < SLOTS
    hits = [meta[m : m + 1, :] == token for m in range(3)]
    into = jnp.where(hits[0] & low, 1.0, 0.0).astype(jnp.bfloat16)
    late = [jnp.where(hit & ~low, 1.0, 0.0).astype(jnp.bfloat16) for hit in hits]
    return main, into, late


def project_kernel(
    sides, place_ref, got_ref, own_ref, other_ref, cosine_ref, sine_ref,
    keys_ref, mine_ref, theirs_ref, mine_turned, theirs_turned,
):
    bf16, f32 = jnp.bfloat16, jnp.float32
    rows = mine_ref.shape[0]
    count = mine_ref.shape[1] // HEAD_DIM
    _, into, _ = arrivals(got_ref, rows)
    done = jnp.dot(into, got_ref[:, : 2 * count * HEAD_DIM], preferred_element_type=f32)
    is_first = jnp.broadcast_to(place_ref[0], (rows, HEAD_DIM)) == 0
    own_tiles, other_tiles = [], []
    for i in range(count):
        even = done[:, 2 * i * HEAD_DIM : (2 * i + 1) * HEAD_DIM]
        odd = done[:, (2 * i + 1) * HEAD_DIM : (2 * i + 2) * HEAD_DIM]
        own = jnp.where(is_first, even, odd).astype(bf16)
        other = jnp.where(is_first, odd, even).astype(bf16)
        own_tiles.append(own)
        other_tiles.append(other)
        turned = lax.rem(place_ref[1] - i + count, count)
        lanes = pl.ds(pl.multiple_of(turned * HEAD_DIM, HEAD_DIM), HEAD_DIM)
        mine_turned[:, lanes] = own
        theirs_turned[:, lanes] = other
    keys = jnp.dot(mine_turned[...], own_ref[...], preferred_element_type=f32)
    keys = keys + jnp.dot(theirs_turned[...], other_ref[...], preferred_element_type=f32)
    for h in range(keys.shape[1] // HEAD_DIM):
        head = keys[:, h * HEAD_DIM : (h + 1) * HEAD_DIM]
        swapped = pltpu.roll(head, HEAD_DIM // 2, 1)
        keys_ref[:, h * HEAD_DIM : (h + 1) * HEAD_DIM] = (
            head * cosine_ref[...] + swapped * sine_ref[...]
        ).astype(bf16)
    source = lax.broadcasted_iota(jnp.int32, (HEAD_DIM, HEAD_DIM), 0)
    target = lax.broadcasted_iota(jnp.int32, (HEAD_DIM, HEAD_DIM), 1)
    part = HEAD_DIM // sides
    wanted = (target % part) // 4 * (4 * sides) + target // part * 4 + target % 4
    order = jnp.where(source == wanted, 1.0, 0.0).astype(bf16)
    for tiles, ref in ((own_tiles, mine_ref), (other_tiles, theirs_ref)):
        moved = jnp.dot(
            jnp.concatenate(tiles, axis=0), order, preferred_element_type=f32
        ).astype(bf16)
        for i in range(count):
            ref[:, i * HEAD_DIM : (i + 1) * HEAD_DIM] = moved[i * rows : (i + 1) * rows]


def rest_kernel(got_ref, queries_ref, values_ref):
    bf16, f32 = jnp.bfloat16, jnp.float32
    rows, width = queries_ref.shape
    main, into, late = arrivals(got_ref, rows)
    first = jnp.dot(into, got_ref[:, width : main * HEAD_DIM], preferred_element_type=f32)
    first_width = first.shape[1]
    queries_ref[:, :first_width] = first.astype(bf16)
    extras = jnp.zeros((rows, main // 3 * HEAD_DIM), f32)
    for m in range(3):
        extras = extras + jnp.dot(
            late[m], tile_columns(got_ref, range(m, main, 3)), preferred_element_type=f32
        )
    extras = extras.astype(bf16)
    queries_ref[:, first_width:] = extras[:, : width - first_width]
    values_ref[...] = extras[:, width - first_width :]


def attend_kernel(
    start_ref, q_ref, k0_ref, k1_ref, k2_ref, pick_ref, prob_ref,
    g0_ref, g1_ref, g2_ref, loss_ref, weight_ref, spot_scr, prob_scr,
):
    bf16, f32 = jnp.bfloat16, jnp.float32
    rows = q_ref.shape[0]
    kv_count = k0_ref.shape[1] // HEAD_DIM
    heads = q_ref.shape[1] // HEAD_DIM
    group = heads // kv_count
    top = pick_ref.shape[1] // heads
    window = SPAN * rows
    scaling = HEAD_DIM ** (-0.5)
    query = lax.broadcasted_iota(jnp.int32, (1, rows), 1).astype(f32)
    start = start_ref[...].astype(f32)
    reach = query - start + 1.0
    picked = pick_ref[...].astype(f32).T
    rest = picked - jnp.floor(picked / reach) * reach
    rest = jnp.where(rest < 0.0, rest + reach, rest)
    rest = jnp.where(rest >= reach, rest - reach, rest)
    spot = start + rest
    spot_scr[...] = jnp.where(spot < 0.0, spot + window, spot)
    prob_all = prob_ref[...].T
    prob_scr[...] = prob_all
    entropy = jnp.sum(prob_all * jnp.log(prob_all), axis=0, keepdims=True)
    spots = lax.broadcasted_iota(jnp.int32, (window, rows), 0).astype(f32)
    across = lax.broadcasted_iota(jnp.int32, (window, rows), 1).astype(f32)
    position = jnp.where(spots <= across, spots, spots - window)
    allowed = position >= start
    near = spots[:rows] <= across[:rows]

    def parted(rows_of):
        low = rows_of[:rows]
        return jnp.concatenate(
            [jnp.where(near, low, 0.0), jnp.where(near, 0.0, low), rows_of[rows:]], axis=0
        ).astype(bf16)

    def one_group(g, loss):
        lanes = pl.ds(pl.multiple_of(g * HEAD_DIM, HEAD_DIM), HEAD_DIM)
        queries = jnp.concatenate(
            [
                q_ref[:, pl.ds(pl.multiple_of((g * group + i) * HEAD_DIM, HEAD_DIM), HEAD_DIM)]
                for i in range(group)
            ],
            axis=0,
        )
        keys = jnp.concatenate([k0_ref[:, lanes], k2_ref[:, lanes], k1_ref[:, lanes]], axis=0)
        dots = lax.dot_general(
            keys, queries, (((1,), (1,)), ((), ())), preferred_element_type=f32
        )
        slopes = []
        for i in range(group):
            mine = dots[:, i * rows : (i + 1) * rows]
            score = (
                jnp.concatenate(
                    [jnp.where(near, mine[:rows], mine[rows : 2 * rows]), mine[2 * rows :]], axis=0
                )
                * scaling
            )
            held = jnp.where(allowed, score, negative)
            peak = jnp.max(held, axis=0, keepdims=True)
            raised = jnp.exp(held - peak)
            total = jnp.sum(raised, axis=0, keepdims=True)
            weight = raised * (1.0 / total)
            labels = pl.ds(pl.multiple_of((g * group + i) * top, top), top)
            spot_rows, prob_rows = spot_scr[labels, :], prob_scr[labels, :]
            table = jnp.zeros((window, rows), f32)
            for k in range(top):
                table = table + jnp.where(
                    spots == spot_rows[k : k + 1], prob_rows[k : k + 1], 0.0
                )
            mass = jnp.sum(prob_rows, axis=0, keepdims=True)
            loss = loss + mass * (peak + jnp.log(total))
            loss = loss - jnp.sum(table * score, axis=0, keepdims=True)
            weight_ref[g, :, i * rows : (i + 1) * rows] = parted(weight)
            slopes.append(parted((weight * mass - table) * (1.0 / heads)))
        grads = jnp.dot(
            jnp.concatenate(slopes, axis=1), queries, preferred_element_type=f32
        ) * scaling
        g0_ref[:, lanes] = grads[:rows]
        g2_ref[:, lanes] = grads[rows : 2 * rows].astype(bf16)
        g1_ref[:, lanes] = grads[2 * rows :].astype(bf16)
        return loss

    loss = lax.fori_loop(0, kv_count, one_group, entropy)
    loss_ref[...] = loss * (1.0 / heads)


def output_kernel(weight_ref, v0_ref, v1_ref, v2_ref, out_ref):
    bf16, f32 = jnp.bfloat16, jnp.float32
    rows = v0_ref.shape[0]
    group = weight_ref.shape[2] // rows
    for g in range(weight_ref.shape[0]):
        lanes = slice(g * HEAD_DIM, (g + 1) * HEAD_DIM)
        values = jnp.concatenate([v0_ref[:, lanes], v2_ref[:, lanes], v1_ref[:, lanes]], axis=0)
        flipped = jnp.dot(
            values.astype(f32).T.astype(bf16), weight_ref[g], preferred_element_type=f32
        )
        for i in range(group):
            h = g * group + i
            out_ref[:, h * HEAD_DIM : (h + 1) * HEAD_DIM] = (
                flipped[:, i * rows : (i + 1) * rows].T.astype(bf16)
            )


def attend(start, queries, keys, pick, prob):
    rows, kv_width = keys[0].shape
    kv_count = kv_width // HEAD_DIM
    group = queries.shape[1] // kv_width
    bf16, f32 = jnp.bfloat16, jnp.float32
    struct = jax.ShapeDtypeStruct
    return pl.pallas_call(
        attend_kernel,
        out_shape=[
            struct((rows, kv_width), f32),
            struct((rows, kv_width), bf16),
            struct((rows, kv_width), bf16),
            struct((1, rows), f32),
            struct((kv_count, (SPAN + 1) * rows, group * rows), bf16),
        ],
        in_specs=whole(7),
        out_specs=whole(5),
        scratch_shapes=[pltpu.VMEM(pick.shape[::-1], f32)] * 2,
        compiler_params=GRANT,
        name="attend",
    )(start.reshape(1, rows), queries, *keys, pick, prob)


def attend_output(weights, values):
    rows = values[0].shape[0]
    heads = weights.shape[0] * weights.shape[2] // rows
    return pl.pallas_call(
        output_kernel,
        out_shape=jax.ShapeDtypeStruct((rows, heads * HEAD_DIM), jnp.bfloat16),
        in_specs=whole(4),
        out_specs=whole()[0],
        compiler_params=GRANT,
        name="attend_output",
    )(weights, *values)


def whole(count=1):
    return [pl.BlockSpec(memory_space=pltpu.VMEM)] * count


def pack_rows(hidden, queries, values, row_target, seq_count):
    rows = hidden.shape[0]
    tiles = (hidden.shape[1] + queries.shape[1] + values.shape[1]) // HEAD_DIM
    main = tiles - tiles // 4
    return pl.pallas_call(
        pack_kernel,
        out_shape=jax.ShapeDtypeStruct((seq_count * 8, (main + 1) * HEAD_DIM), jnp.bfloat16),
        in_specs=whole(4),
        out_specs=whole()[0],
        compiler_params=GRANT,
        name="pack_rows",
    )(row_target.reshape(1, rows), hidden, queries, values)


def project(got, place_of, own_half, other_half, cosine, sine, sides):
    rows, (width, kv_width) = cosine.shape[0], own_half.shape
    struct = jax.ShapeDtypeStruct
    return pl.pallas_call(
        functools.partial(project_kernel, sides),
        out_shape=[struct((rows, w), jnp.bfloat16) for w in (kv_width, width, width)],
        in_specs=[pl.BlockSpec(memory_space=pltpu.SMEM)] + whole(5),
        out_specs=whole(3),
        scratch_shapes=[pltpu.VMEM((rows, width), jnp.bfloat16)] * 2,
        compiler_params=GRANT,
        name="project",
    )(place_of, got, own_half, other_half, cosine, sine)


def unpack_rest(got, rows, width, kv_width):
    return pl.pallas_call(
        rest_kernel,
        out_shape=[jax.ShapeDtypeStruct((rows, w), jnp.bfloat16) for w in (width, kv_width)],
        in_specs=whole(),
        out_specs=whole(2),
        compiler_params=GRANT,
        name="unpack_rest",
    )(got)


def step(
    hidden, queries, values, row_target, key_weight, dialogue_lengths, teacher_pick, teacher_prob
):
    bf16, f32 = jnp.bfloat16, jnp.float32
    local_rows, width = hidden.shape
    seq_count = lax.axis_size(SEQ)
    seq_index = lax.axis_index(SEQ)
    lines = lax.axis_size("y")
    device_count = seq_count * lines * lax.axis_size("core")
    kv_width = values.shape[1]

    place_of = jnp.stack([lax.axis_index("core"), lax.axis_index("y")]).astype(jnp.int32)

    plane_rows = exchange(jnp.broadcast_to(key_weight, (seq_count,) + key_weight.shape), SEQ)
    plane_rows = plane_rows.reshape(local_rows, kv_width)
    turned = [plane_rows]
    for by in range(1, lines):
        turned.append(line_shift(plane_rows, by))
    own_half = jnp.concatenate(turned, axis=0)
    other_half = core_swap(own_half)

    parcels = pack_rows(hidden, queries, values, row_target, seq_count)
    received = exchange(parcels.reshape(seq_count, 8, -1), SEQ)
    got = received.reshape(seq_count * 8, -1)
    positions = seq_index * local_rows + jnp.arange(local_rows, dtype=jnp.int32)
    cosine, sine = turn_angles(positions)
    keys_seq, mine, theirs = project(
        got,
        place_of,
        own_half,
        other_half,
        jnp.concatenate([cosine[:, 0], cosine[:, 0]], axis=1),
        jnp.concatenate([-sine[:, 0], sine[:, 0]], axis=1),
        lax.axis_size(ACROSS),
    )
    queries_seq, values_seq = unpack_rest(got, local_rows, width, kv_width)

    starts = dialogue_starts(dialogue_lengths[0], positions)
    near_keys = [seq_shift(keys_seq, by) for by in range(1, SPAN + 1)]
    values_late, *near_keys = lax.optimization_barrier((values_seq, *near_keys))
    values_all = [values_seq]
    for by in range(1, SPAN + 1):
        values_all.append(seq_shift(values_late, by))
    own_grad, grad_1, grad_2, token_loss, weights = attend(
        starts - seq_index * local_rows,
        queries_seq,
        [keys_seq] + near_keys,
        teacher_pick,
        teacher_prob,
    )
    theirs, own_grad = lax.optimization_barrier((theirs, own_grad))
    partner = core_swap(theirs)
    rotated_grad = (
        own_grad + seq_shift(grad_1, -1).astype(f32) + seq_shift(grad_2, -2).astype(f32)
    )
    key_grad = rotate(rotated_grad, cosine, -sine).astype(bf16)

    inverse_root = (local_rows * device_count) ** (-0.5)

    def term(columns, grads):
        return jnp.einsum("td,tc->dc", columns, grads, preferred_element_type=f32)

    summed = (term(mine, key_grad) + term(partner, core_swap(key_grad))).astype(bf16)
    sides = lax.axis_size(ACROSS)
    pieces = jnp.transpose(summed.reshape(lines, sides, -1, kv_width), (1, 0, 2, 3))
    pieces = pieces.reshape(sides, -1, kv_width)
    line = jnp.sum(exchange(pieces, ACROSS).astype(f32), axis=0).astype(bf16)
    attn_out = attend_output(weights, values_all)
    last = exchange(line.reshape(-1, 4, kv_width), ("y", "z"))
    weight_grad = jnp.sum(last.astype(f32), axis=0) * inverse_root
    return (attn_out, token_loss.reshape(local_rows), weight_grad)


def solution(mesh):
    fine = Mesh(np.asarray(mesh.devices).reshape(8, 2, 8, 2, 2), EVERY)
    pack = ("y", "core")
    placed = (
        P(EVERY, None),
        P(EVERY, None),
        P(EVERY, None),
        P(EVERY),
        P(EVERY, None),
        P(pack, None),
        P(EVERY, None),
        P(EVERY, None),
    )
    return jax.shard_map(
        step,
        mesh=fine,
        in_specs=placed,
        out_specs=(P(EVERY, None), P(EVERY), P(EVERY, None)),
        check_vma=False,
    )
```

profile of v0, /device:TPU:66, one launch (start us, length us, event | category | flops | bytes accessed | tf_op | source)
XLA Modules:
  0.0 159.5 jit_solution(16680232769146778725)
XLA Ops:
  0.6 1.4 broadcast_in_dim.26
  2.0 12.6 %all-to-all-start.1 = ((bf16[32,4,512]{2,1,0:T(4,128)(2,1)}), bf16[32,4,512]{2,1,0:T(4,128)(2,1)S(1)}, u32[]{:S(2)}, u32[]{:S(2)}) async-start(bf16[32,4,512]{2,1,0:T(4,128)(2,1)} %broadcast_in_dim.26), calls=%async_computation.1 | async-start | bytes 262144 | tf_op jit(solution)/shard_map/all_to_all | solution.py:28
  14.6 1.0 copy-done.1
  15.6 1.0 copy-done.2
  16.7 0.9 copy-done.3
  17.6 0.7 copy-done.6
  18.2 0.8 pack_rows.1
  19.1 1.3 copy-done
  20.3 3.0 %all-to-all-done.1 = bf16[32,4,512]{2,1,0:T(4,128)(2,1)S(1)} async-done(((bf16[32,4,512]{2,1,0:T(4,128)(2,1)}), bf16[32,4,512]{2,1,0:T(4,128)(2,1)S(1)}, u32[]{:S(2)}, u32[]{:S(2)}) %all-to-all-start.1) | async-done | bytes 131104 | tf_op jit(solution)/shard_map/all_to_all | solution.py:28
  23.3 6.8 %all-to-all-start = ((bf16[32,8,3584]{2,1,0:T(8,128)(2,1)}), bf16[32,8,3584]{2,1,0:T(8,128)(2,1)S(1)}, u32[]{:S(2)}, u32[]{:S(2)}) async-start(bf16[32,8,3584]{2,1,0:T(8,128)(2,1)} %bitcast.24), calls=%async_computation | async-start | bytes 3670016 | tf_op jit(solution)/shard_map/all_to_all | solution.py:28
  30.2 3.5 %collective-permute-start = (bf16[128,512]{1,0:T(8,128)(2,1)S(1)}, bf16[128,512]{1,0:T(8,128)(2,1)S(1)}, u32[]{:S(2)}, u32[]{:S(2)}) collective-permute-start(bf16[128,512]{1,0:T(8,128)(2,1)S(1)} %reshape.135), channel_id=1, source_target_pairs={{0,64},{64,128},{128,192},{192,256},{256,320},{320,384},{384,448},... | collective-permute-start | bytes 393224 | tf_op jit(solution)/shard_map/ppermute | solution.py:39
  33.6 4.5 %collective-permute-start.1 = (bf16[128,512]{1,0:T(8,128)(2,1)S(1)}, bf16[128,512]{1,0:T(8,128)(2,1)S(1)}, u32[]{:S(2)}, u32[]{:S(2)}) collective-permute-start(bf16[128,512]{1,0:T(8,128)(2,1)S(1)} %reshape.135), channel_id=1, source_target_pairs={{0,128},{64,192},{128,256},{192,320},{256,384},{320,448},{384,0},{... | collective-permute-start | bytes 393224 | tf_op jit(solution)/shard_map/ppermute | solution.py:39
  38.2 4.9 %collective-permute-start.2 = (bf16[128,512]{1,0:T(8,128)(2,1)S(1)}, bf16[128,512]{1,0:T(8,128)(2,1)S(1)}, u32[]{:S(2)}, u32[]{:S(2)}) collective-permute-start(bf16[128,512]{1,0:T(8,128)(2,1)S(1)} %reshape.135), channel_id=1, source_target_pairs={{0,192},{64,256},{128,320},{192,384},{256,448},{320,0},{384,64},{4... | collective-permute-start | bytes 393224 | tf_op jit(solution)/shard_map/ppermute | solution.py:39
  43.1 3.8 %collective-permute-start.3 = (bf16[128,512]{1,0:T(8,128)(2,1)S(1)}, bf16[128,512]{1,0:T(8,128)(2,1)S(1)}, u32[]{:S(2)}, u32[]{:S(2)}) collective-permute-start(bf16[128,512]{1,0:T(8,128)(2,1)S(1)} %reshape.135), channel_id=1, source_target_pairs={{0,256},{64,320},{128,384},{192,448},{256,0},{320,64},{384,128},{4... | collective-permute-start | bytes 393224 | tf_op jit(solution)/shard_map/ppermute | solution.py:39
  46.9 5.2 %collective-permute-start.4 = (bf16[128,512]{1,0:T(8,128)(2,1)S(1)}, bf16[128,512]{1,0:T(8,128)(2,1)S(1)}, u32[]{:S(2)}, u32[]{:S(2)}) collective-permute-start(bf16[128,512]{1,0:T(8,128)(2,1)S(1)} %reshape.135), channel_id=1, source_target_pairs={{0,320},{64,384},{128,448},{192,0},{256,64},{320,128},{384,192},{4... | collective-permute-start | bytes 393224 | tf_op jit(solution)/shard_map/ppermute | solution.py:39
  52.1 5.3 %collective-permute-start.5 = (bf16[128,512]{1,0:T(8,128)(2,1)S(1)}, bf16[128,512]{1,0:T(8,128)(2,1)S(1)}, u32[]{:S(2)}, u32[]{:S(2)}) collective-permute-start(bf16[128,512]{1,0:T(8,128)(2,1)S(1)} %reshape.135), channel_id=1, source_target_pairs={{0,384},{64,448},{128,0},{192,64},{256,128},{320,192},{384,256},{4... | collective-permute-start | bytes 393224 | tf_op jit(solution)/shard_map/ppermute | solution.py:39
  57.4 3.3 %collective-permute-start.6 = (bf16[128,512]{1,0:T(8,128)(2,1)S(1)}, bf16[128,512]{1,0:T(8,128)(2,1)S(1)}, u32[]{:S(2)}, u32[]{:S(2)}) collective-permute-start(bf16[128,512]{1,0:T(8,128)(2,1)S(1)} %reshape.135), channel_id=1, source_target_pairs={{0,448},{64,0},{128,64},{192,128},{256,192},{320,256},{384,320},{4... | collective-permute-start | bytes 393224 | tf_op jit(solution)/shard_map/ppermute | solution.py:39
  60.7 5.0 %collective-permute-done.4 = bf16[128,512]{1,0:T(8,128)(2,1)S(1)} collective-permute-done((bf16[128,512]{1,0:T(8,128)(2,1)S(1)}, bf16[128,512]{1,0:T(8,128)(2,1)S(1)}, u32[]{:S(2)}, u32[]{:S(2)}) %collective-permute-start.4) | collective-permute-done | bytes 131104 | tf_op jit(solution)/shard_map/ppermute | solution.py:39
  65.7 3.0 %collective-permute-done.5 = bf16[128,512]{1,0:T(8,128)(2,1)S(1)} collective-permute-done((bf16[128,512]{1,0:T(8,128)(2,1)S(1)}, bf16[128,512]{1,0:T(8,128)(2,1)S(1)}, u32[]{:S(2)}, u32[]{:S(2)}) %collective-permute-start.5) | collective-permute-done | bytes 131104 | tf_op jit(solution)/shard_map/ppermute | solution.py:39
  68.7 1.9 %collective-permute-done.6 = bf16[128,512]{1,0:T(8,128)(2,1)S(1)} collective-permute-done((bf16[128,512]{1,0:T(8,128)(2,1)S(1)}, bf16[128,512]{1,0:T(8,128)(2,1)S(1)}, u32[]{:S(2)}, u32[]{:S(2)}) %collective-permute-start.6) | collective-permute-done | bytes 131104 | tf_op jit(solution)/shard_map/ppermute | solution.py:39
  70.7 1.9 %collective-permute-start.7 = (bf16[1024,512]{1,0:T(8,128)(2,1)S(1)}, bf16[1024,512]{1,0:T(8,128)(2,1)}, u32[]{:S(2)}, u32[]{:S(2)}) collective-permute-start(bf16[1024,512]{1,0:T(8,128)(2,1)S(1)} %constant_dynamic-update-slice_fusion.own_ref), channel_id=1, source_target_pairs={{0,32},{32,0},{1,33},{33,1},{2,34},{34,2},{3,35},{35,3},{4,36},{36... | collective-permute-start | bytes 3145736 | tf_op jit(solution)/shard_map/ppermute | solution.py:43
  73.0 0.3 fusion
  73.4 0.5 copy-done.9
  74.1 1.2 collective-permute-done.7.other_ref
  75.4 2.2 %project.1 = (bf16[128,512]{1,0:T(8,128)(2,1)S(1)}, bf16[128,1024]{1,0:T(8,128)(2,1)S(1)}, bf16[128,1024]{1,0:T(8,128)(2,1)S(1)}) custom-call(s32[2]{0:T(128)S(1)} %pad_add_fusion.place_ref, bf16[256,3584]{1,0:T(8,128)(2,1)S(1)} %bitcast.22, bf16[1024,512]{1,0:T(8,128)(2,1)S(1)} %constant_dynamic-update-slice_fusion.own_ref, ...), custom_call_target="tpu_custom_call" | custom-call | tf_op jit(solution)/shard_map/project/pallas_call | solution.py:348
  77.6 3.4 %collective-permute-start.8 = (bf16[128,512]{1,0:T(8,128)(2,1)S(1)}, bf16[128,512]{1,0:T(8,128)(2,1)S(1)}, u32[]{:S(2)}, u32[]{:S(2)}) collective-permute-start(bf16[128,512]{1,0:T(8,128)(2,1)S(1)} %get-tuple-element.19.k0_ref), channel_id=1, source_target_pairs={{0,1},{1,2},{2,3},{3,4},{4,5},{5,6},{6,7},{7,8},{8,9},{9,10},{10,1... | collective-permute-start | bytes 393224 | tf_op jit(solution)/shard_map/ppermute | solution.py:34
  81.0 4.0 %collective-permute-start.9 = (bf16[128,512]{1,0:T(8,128)(2,1)S(1)}, bf16[128,512]{1,0:T(8,128)(2,1)S(1)}, u32[]{:S(2)}, u32[]{:S(2)}) collective-permute-start(bf16[128,512]{1,0:T(8,128)(2,1)S(1)} %get-tuple-element.19.k0_ref), channel_id=1, source_target_pairs={{0,2},{1,3},{2,4},{3,5},{4,6},{5,7},{6,8},{7,9},{8,10},{9,11},{10,... | collective-permute-start | bytes 393224 | tf_op jit(solution)/shard_map/ppermute | solution.py:34
  85.0 0.6 unpack_rest.1
  85.6 4.9 %collective-permute-done.9.k2_ref = bf16[128,512]{1,0:T(8,128)(2,1)S(1)} collective-permute-done((bf16[128,512]{1,0:T(8,128)(2,1)S(1)}, bf16[128,512]{1,0:T(8,128)(2,1)S(1)}, u32[]{:S(2)}, u32[]{:S(2)}) %collective-permute-start.9) | collective-permute-done | bytes 131104 | tf_op jit(solution)/shard_map/ppermute | solution.py:34
  90.5 4.8 %attend.1 = (f32[128,512]{1,0:T(8,128)S(1)}, bf16[128,512]{1,0:T(8,128)(2,1)S(1)}, bf16[128,512]{1,0:T(8,128)(2,1)S(1)}, f32[1,128]{1,0:T(1,128)}, bf16[4,384,512]{2,1,0:T(8,128)(2,1)S(1)}) custom-call(s32[1,128]{1,0:T(1,128)S(1)} %subtract_bitcast_fusion.start_ref, bf16[128,2048]{1,0:T(8,128)(2,1)S(1)} %get-tuple-element.18.q_ref, ...), custom_call_target="tpu_custom_call" | custom-call | tf_op jit(solution)/shard_map/attend/pallas_call | solution.py:297
  95.3 3.1 %collective-permute-start.13 = (bf16[128,512]{1,0:T(8,128)(2,1)S(1)}, bf16[128,512]{1,0:T(8,128)(2,1)S(1)}, u32[]{:S(2)}, u32[]{:S(2)}) collective-permute-start(bf16[128,512]{1,0:T(8,128)(2,1)S(1)} %get-tuple-element.31), channel_id=1, source_target_pairs={{2,0},{3,1},{4,2},{5,3},{6,4},{7,5},{8,6},{9,7},{10,8},{11,9},{12,... | collective-permute-start | bytes 393224 | tf_op jit(solution)/shard_map/ppermute | solution.py:34
  98.4 3.1 %collective-permute-start.12 = (bf16[128,512]{1,0:T(8,128)(2,1)S(1)}, bf16[128,512]{1,0:T(8,128)(2,1)S(1)}, u32[]{:S(2)}, u32[]{:S(2)}) collective-permute-start(bf16[128,512]{1,0:T(8,128)(2,1)S(1)} %get-tuple-element.30), channel_id=1, source_target_pairs={{1,0},{2,1},{3,2},{4,3},{5,4},{6,5},{7,6},{8,7},{9,8},{10,9},{11,1... | collective-permute-start | bytes 393224 | tf_op jit(solution)/shard_map/ppermute | solution.py:34
  101.5 1.9 %collective-permute-start.14 = (bf16[128,1024]{1,0:T(8,128)(2,1)S(1)}, bf16[128,1024]{1,0:T(8,128)(2,1)S(1)}, u32[]{:S(2)}, u32[]{:S(2)}) collective-permute-start(bf16[128,1024]{1,0:T(8,128)(2,1)S(1)} %get-tuple-element.32), channel_id=1, source_target_pairs={{0,32},{32,0},{1,33},{33,1},{2,34},{34,2},{3,35},{35,3},{4,36},{36... | collective-permute-start | bytes 786440 | tf_op jit(solution)/shard_map/ppermute | solution.py:43
  103.4 1.7 %collective-permute-done.13 = bf16[128,512]{1,0:T(8,128)(2,1)S(1)} collective-permute-done((bf16[128,512]{1,0:T(8,128)(2,1)S(1)}, bf16[128,512]{1,0:T(8,128)(2,1)S(1)}, u32[]{:S(2)}, u32[]{:S(2)}) %collective-permute-start.13) | collective-permute-done | bytes 131104 | tf_op jit(solution)/shard_map/ppermute | solution.py:34
  105.1 0.8 collective-permute-done.12
  106.1 0.3 subtract_convert_fusion
  106.6 1.9 %collective-permute-start.15 = (bf16[128,512]{1,0:T(8,128)(2,1)S(1)}, bf16[128,512]{1,0:T(8,128)(2,1)S(1)}, u32[]{:S(2)}, u32[]{:S(2)}) collective-permute-start(bf16[128,512]{1,0:T(8,128)(2,1)S(1)} %bitcast.30), channel_id=1, source_target_pairs={{0,32},{32,0},{1,33},{33,1},{2,34},{34,2},{3,35},{35,3},{4,36},{36... | collective-permute-start | bytes 393224 | tf_op jit(solution)/shard_map/ppermute | solution.py:43
  108.5 1.3 collective-permute-done.15
  109.8 0.5 fusion.2
  110.3 0.5 add_convert_fusion
  110.8 20.0 %all_to_all.20 = bf16[4,256,512]{2,1,0:T(8,128)(2,1)S(1)} all-to-all(bf16[4,256,512]{2,1,0:T(8,128)(2,1)S(1)} %bitcast.27), channel_id=1, replica_groups=mesh['y'=8,'core'=2,'z'=8,'xh'=2,'xl'=2] {'xh','xl'}, dimensions={0} | all-to-all | bytes 2097152 | tf_op jit(solution)/shard_map/all_to_all | solution.py:28
  131.1 0.8 reshape.140
  131.8 11.1 %all-to-all-start.3 = ((bf16[64,4,512]{2,1,0:T(4,128)(2,1)}), bf16[64,4,512]{2,1,0:T(4,128)(2,1)S(1)}, u32[]{:S(2)}, u32[]{:S(2)}) async-start(bf16[64,4,512]{2,1,0:T(4,128)(2,1)} %reshape.140), calls=%async_computation.3 | async-start | bytes 524288 | tf_op jit(solution)/shard_map/all_to_all | solution.py:28
  142.9 2.1 %collective-permute-start.10 = (bf16[128,512]{1,0:T(8,128)(2,1)S(1)}, bf16[128,512]{1,0:T(8,128)(2,1)S(1)}, u32[]{:S(2)}, u32[]{:S(2)}) collective-permute-start(bf16[128,512]{1,0:T(8,128)(2,1)S(1)} %get-tuple-element.24.v0_ref), channel_id=1, source_target_pairs={{0,1},{1,2},{2,3},{3,4},{4,5},{5,6},{6,7},{7,8},{8,9},{9,10},{10,1... | collective-permute-start | bytes 393224 | tf_op jit(solution)/shard_map/ppermute | solution.py:34
  145.1 6.1 %collective-permute-start.11 = (bf16[128,512]{1,0:T(8,128)(2,1)S(1)}, bf16[128,512]{1,0:T(8,128)(2,1)S(1)}, u32[]{:S(2)}, u32[]{:S(2)}) collective-permute-start(bf16[128,512]{1,0:T(8,128)(2,1)S(1)} %get-tuple-element.24.v0_ref), channel_id=1, source_target_pairs={{0,2},{1,3},{2,4},{3,5},{4,6},{5,7},{6,8},{7,9},{8,10},{9,11},{10,... | collective-permute-start | bytes 393224 | tf_op jit(solution)/shard_map/ppermute | solution.py:34
  151.2 6.3 %collective-permute-done.11.v2_ref = bf16[128,512]{1,0:T(8,128)(2,1)S(1)} collective-permute-done((bf16[128,512]{1,0:T(8,128)(2,1)S(1)}, bf16[128,512]{1,0:T(8,128)(2,1)S(1)}, u32[]{:S(2)}, u32[]{:S(2)}) %collective-permute-start.11) | collective-permute-done | bytes 131104 | tf_op jit(solution)/shard_map/ppermute | solution.py:34
  157.5 1.4 attend_output.1
  158.9 0.6 broadcast_multiply_fusion
  (53 shorter events, 1.6 us)
Async XLA Ops:
  2.0 21.3 %all-to-all-start.1 = ((bf16[32,4,512]{2,1,0:T(4,128)(2,1)}), bf16[32,4,512]{2,1,0:T(4,128)(2,1)S(1)}, u32[]{:S(2)}, u32[]{:S(2)}) async-start(bf16[32,4,512]{2,1,0:T(4,128)(2,1)} %broadcast_in_dim.26), calls=%async_computation.1 | async-start | bytes 262144 | tf_op jit(solution)/shard_map/all_to_all | solution.py:28
  14.6 1.0 copy-start.1
  15.6 1.0 copy-start.2
  16.7 0.9 copy-start.3
  17.6 0.7 copy-start.6
  19.0 1.3 copy-start
  23.3 52.0 %all-to-all-start = ((bf16[32,8,3584]{2,1,0:T(8,128)(2,1)}), bf16[32,8,3584]{2,1,0:T(8,128)(2,1)S(1)}, u32[]{:S(2)}, u32[]{:S(2)}) async-start(bf16[32,8,3584]{2,1,0:T(8,128)(2,1)} %bitcast.24), calls=%async_computation | async-start | bytes 3670016 | tf_op jit(solution)/shard_map/all_to_all | solution.py:28
  30.1 42.5 %copy-start.11 = (s32[1,64]{1,0:T(1,128)S(1)}, s32[1,64]{1,0:T(1,128)}, u32[]{:S(2)}) copy-start(s32[1,64]{1,0:T(1,128)} %param.13) | copy-start | bytes 772
  30.2 21.9 %collective-permute-start = (bf16[128,512]{1,0:T(8,128)(2,1)S(1)}, bf16[128,512]{1,0:T(8,128)(2,1)S(1)}, u32[]{:S(2)}, u32[]{:S(2)}) collective-permute-start(bf16[128,512]{1,0:T(8,128)(2,1)S(1)} %reshape.135), channel_id=1, source_target_pairs={{0,64},{64,128},{128,192},{192,256},{256,320},{320,384},{384,448},... | collective-permute-start | bytes 393224 | tf_op jit(solution)/shard_map/ppermute | solution.py:39
  33.6 23.7 %collective-permute-start.1 = (bf16[128,512]{1,0:T(8,128)(2,1)S(1)}, bf16[128,512]{1,0:T(8,128)(2,1)S(1)}, u32[]{:S(2)}, u32[]{:S(2)}) collective-permute-start(bf16[128,512]{1,0:T(8,128)(2,1)S(1)} %reshape.135), channel_id=1, source_target_pairs={{0,128},{64,192},{128,256},{192,320},{256,384},{320,448},{384,0},{... | collective-permute-start | bytes 393224 | tf_op jit(solution)/shard_map/ppermute | solution.py:39
  38.2 22.5 %collective-permute-start.2 = (bf16[128,512]{1,0:T(8,128)(2,1)S(1)}, bf16[128,512]{1,0:T(8,128)(2,1)S(1)}, u32[]{:S(2)}, u32[]{:S(2)}) collective-permute-start(bf16[128,512]{1,0:T(8,128)(2,1)S(1)} %reshape.135), channel_id=1, source_target_pairs={{0,192},{64,256},{128,320},{192,384},{256,448},{320,0},{384,64},{4... | collective-permute-start | bytes 393224 | tf_op jit(solution)/shard_map/ppermute | solution.py:39
  43.1 17.6 %collective-permute-start.3 = (bf16[128,512]{1,0:T(8,128)(2,1)S(1)}, bf16[128,512]{1,0:T(8,128)(2,1)S(1)}, u32[]{:S(2)}, u32[]{:S(2)}) collective-permute-start(bf16[128,512]{1,0:T(8,128)(2,1)S(1)} %reshape.135), channel_id=1, source_target_pairs={{0,256},{64,320},{128,384},{192,448},{256,0},{320,64},{384,128},{4... | collective-permute-start | bytes 393224 | tf_op jit(solution)/shard_map/ppermute | solution.py:39
  46.9 18.8 %collective-permute-start.4 = (bf16[128,512]{1,0:T(8,128)(2,1)S(1)}, bf16[128,512]{1,0:T(8,128)(2,1)S(1)}, u32[]{:S(2)}, u32[]{:S(2)}) collective-permute-start(bf16[128,512]{1,0:T(8,128)(2,1)S(1)} %reshape.135), channel_id=1, source_target_pairs={{0,320},{64,384},{128,448},{192,0},{256,64},{320,128},{384,192},{4... | collective-permute-start | bytes 393224 | tf_op jit(solution)/shard_map/ppermute | solution.py:39
  52.1 16.6 %collective-permute-start.5 = (bf16[128,512]{1,0:T(8,128)(2,1)S(1)}, bf16[128,512]{1,0:T(8,128)(2,1)S(1)}, u32[]{:S(2)}, u32[]{:S(2)}) collective-permute-start(bf16[128,512]{1,0:T(8,128)(2,1)S(1)} %reshape.135), channel_id=1, source_target_pairs={{0,384},{64,448},{128,0},{192,64},{256,128},{320,192},{384,256},{4... | collective-permute-start | bytes 393224 | tf_op jit(solution)/shard_map/ppermute | solution.py:39
  57.4 13.3 %collective-permute-start.6 = (bf16[128,512]{1,0:T(8,128)(2,1)S(1)}, bf16[128,512]{1,0:T(8,128)(2,1)S(1)}, u32[]{:S(2)}, u32[]{:S(2)}) collective-permute-start(bf16[128,512]{1,0:T(8,128)(2,1)S(1)} %reshape.135), channel_id=1, source_target_pairs={{0,448},{64,0},{128,64},{192,128},{256,192},{320,256},{384,320},{4... | collective-permute-start | bytes 393224 | tf_op jit(solution)/shard_map/ppermute | solution.py:39
  70.7 4.7 %collective-permute-start.7 = (bf16[1024,512]{1,0:T(8,128)(2,1)S(1)}, bf16[1024,512]{1,0:T(8,128)(2,1)}, u32[]{:S(2)}, u32[]{:S(2)}) collective-permute-start(bf16[1024,512]{1,0:T(8,128)(2,1)S(1)} %constant_dynamic-update-slice_fusion.own_ref), channel_id=1, source_target_pairs={{0,32},{32,0},{1,33},{33,1},{2,34},{34,2},{3,35},{35,3},{4,36},{36... | collective-permute-start | bytes 3145736 | tf_op jit(solution)/shard_map/ppermute | solution.py:43
  73.3 0.6 copy-start.9
  73.3 2.0 %copy-start.7 = (f32[128,64]{1,0:T(8,128)}, f32[128,64]{1,0:T(8,128)S(1)}, u32[]{:S(2)}) copy-start(f32[128,64]{1,0:T(8,128)S(1)} %get-tuple-element.35) | copy-start | bytes 98308
  75.3 15.2 %copy-start.4 = (s32[128,128]{1,0:T(8,128)S(1)}, s32[128,128]{1,0:T(8,128)}, u32[]{:S(2)}) copy-start(s32[128,128]{1,0:T(8,128)} %pick_ref.1) | copy-start | bytes 196612
  75.3 15.2 %copy-start.5 = (f32[128,128]{1,0:T(8,128)S(1)}, f32[128,128]{1,0:T(8,128)}, u32[]{:S(2)}) copy-start(f32[128,128]{1,0:T(8,128)} %prob_ref.1) | copy-start | bytes 196612
  77.6 8.0 %collective-permute-start.8 = (bf16[128,512]{1,0:T(8,128)(2,1)S(1)}, bf16[128,512]{1,0:T(8,128)(2,1)S(1)}, u32[]{:S(2)}, u32[]{:S(2)}) collective-permute-start(bf16[128,512]{1,0:T(8,128)(2,1)S(1)} %get-tuple-element.19.k0_ref), channel_id=1, source_target_pairs={{0,1},{1,2},{2,3},{3,4},{4,5},{5,6},{6,7},{7,8},{8,9},{9,10},{10,1... | collective-permute-start | bytes 393224 | tf_op jit(solution)/shard_map/ppermute | solution.py:34
  81.0 9.6 %collective-permute-start.9 = (bf16[128,512]{1,0:T(8,128)(2,1)S(1)}, bf16[128,512]{1,0:T(8,128)(2,1)S(1)}, u32[]{:S(2)}, u32[]{:S(2)}) collective-permute-start(bf16[128,512]{1,0:T(8,128)(2,1)S(1)} %get-tuple-element.19.k0_ref), channel_id=1, source_target_pairs={{0,2},{1,3},{2,4},{3,5},{4,6},{5,7},{6,8},{7,9},{8,10},{9,11},{10,... | collective-permute-start | bytes 393224 | tf_op jit(solution)/shard_map/ppermute | solution.py:34
  85.0 21.1 %copy-start.8 = (f32[128,64]{1,0:T(8,128)S(1)}, f32[128,64]{1,0:T(8,128)}, u32[]{:S(2)}) copy-start(f32[128,64]{1,0:T(8,128)} %copy-done.7) | copy-start | bytes 98308
  85.0 21.1 %copy-start.10 = (f32[128,64]{1,0:T(8,128)S(1)}, f32[128,64]{1,0:T(8,128)}, u32[]{:S(2)}) copy-start(f32[128,64]{1,0:T(8,128)} %copy-done.9) | copy-start | bytes 98308
  95.3 9.8 %collective-permute-start.13 = (bf16[128,512]{1,0:T(8,128)(2,1)S(1)}, bf16[128,512]{1,0:T(8,128)(2,1)S(1)}, u32[]{:S(2)}, u32[]{:S(2)}) collective-permute-start(bf16[128,512]{1,0:T(8,128)(2,1)S(1)} %get-tuple-element.31), channel_id=1, source_target_pairs={{2,0},{3,1},{4,2},{5,3},{6,4},{7,5},{8,6},{9,7},{10,8},{11,9},{12,... | collective-permute-start | bytes 393224 | tf_op jit(solution)/shard_map/ppermute | solution.py:34
  98.4 7.5 %collective-permute-start.12 = (bf16[128,512]{1,0:T(8,128)(2,1)S(1)}, bf16[128,512]{1,0:T(8,128)(2,1)S(1)}, u32[]{:S(2)}, u32[]{:S(2)}) collective-permute-start(bf16[128,512]{1,0:T(8,128)(2,1)S(1)} %get-tuple-element.30), channel_id=1, source_target_pairs={{1,0},{2,1},{3,2},{4,3},{5,4},{6,5},{7,6},{8,7},{9,8},{10,9},{11,1... | collective-permute-start | bytes 393224 | tf_op jit(solution)/shard_map/ppermute | solution.py:34
  101.5 7.0 %collective-permute-start.14 = (bf16[128,1024]{1,0:T(8,128)(2,1)S(1)}, bf16[128,1024]{1,0:T(8,128)(2,1)S(1)}, u32[]{:S(2)}, u32[]{:S(2)}) collective-permute-start(bf16[128,1024]{1,0:T(8,128)(2,1)S(1)} %get-tuple-element.32), channel_id=1, source_target_pairs={{0,32},{32,0},{1,33},{33,1},{2,34},{34,2},{3,35},{35,3},{4,36},{36... | collective-permute-start | bytes 786440 | tf_op jit(solution)/shard_map/ppermute | solution.py:43
  106.6 3.2 %collective-permute-start.15 = (bf16[128,512]{1,0:T(8,128)(2,1)S(1)}, bf16[128,512]{1,0:T(8,128)(2,1)S(1)}, u32[]{:S(2)}, u32[]{:S(2)}) collective-permute-start(bf16[128,512]{1,0:T(8,128)(2,1)S(1)} %bitcast.30), channel_id=1, source_target_pairs={{0,32},{32,0},{1,33},{33,1},{2,34},{34,2},{3,35},{35,3},{4,36},{36... | collective-permute-start | bytes 393224 | tf_op jit(solution)/shard_map/ppermute | solution.py:43
  131.8 27.0 %all-to-all-start.3 = ((bf16[64,4,512]{2,1,0:T(4,128)(2,1)}), bf16[64,4,512]{2,1,0:T(4,128)(2,1)S(1)}, u32[]{:S(2)}, u32[]{:S(2)}) async-start(bf16[64,4,512]{2,1,0:T(4,128)(2,1)} %reshape.140), calls=%async_computation.3 | async-start | bytes 524288 | tf_op jit(solution)/shard_map/all_to_all | solution.py:28
  142.9 8.3 %collective-permute-start.10 = (bf16[128,512]{1,0:T(8,128)(2,1)S(1)}, bf16[128,512]{1,0:T(8,128)(2,1)S(1)}, u32[]{:S(2)}, u32[]{:S(2)}) collective-permute-start(bf16[128,512]{1,0:T(8,128)(2,1)S(1)} %get-tuple-element.24.v0_ref), channel_id=1, source_target_pairs={{0,1},{1,2},{2,3},{3,4},{4,5},{5,6},{6,7},{7,8},{8,9},{9,10},{10,1... | collective-permute-start | bytes 393224 | tf_op jit(solution)/shard_map/ppermute | solution.py:34
  145.1 12.4 %collective-permute-start.11 = (bf16[128,512]{1,0:T(8,128)(2,1)S(1)}, bf16[128,512]{1,0:T(8,128)(2,1)S(1)}, u32[]{:S(2)}, u32[]{:S(2)}) collective-permute-start(bf16[128,512]{1,0:T(8,128)(2,1)S(1)} %get-tuple-element.24.v0_ref), channel_id=1, source_target_pairs={{0,2},{1,3},{2,4},{3,5},{4,6},{5,7},{6,8},{7,9},{8,10},{9,11},{10,... | collective-permute-start | bytes 393224 | tf_op jit(solution)/shard_map/ppermute | solution.py:34
where the time goes:
time: 160 us
  starting transfers between devices  88.3 us (55%)
  waiting for transfers between devices  29.1 us (18%)
  blocking collectives  20 us (12%)
  Pallas kernels  9.76 us (6%)
  local copies, waits for them, and re-layouts  8.01 us (5%)
  other arithmetic  2.29 us (1%)
    all_to_all x3, starting transfers between devices, exchange(): return lax.all_to_all(pieces, axes, split_axis=0, concat_axis=0, tiled=True)  30.4 us
    ppermute x7, starting transfers between devices, line_shift(): lax.ppermute(shard, 'y', [(i, (i + by) % devices) for i in range(devices)])  30.4 us
    ppermute x6, starting transfers between devices, seq_shift(): return lax.ppermute(shard, SEQ, pairs)  21.7 us
    all_to_all x1, blocking collectives, exchange(): return lax.all_to_all(pieces, axes, split_axis=0, concat_axis=0, tiled=True)  20 us
    ppermute x6, waiting for transfers between devices, seq_shift(): return lax.ppermute(shard, SEQ, pairs)  13.7 us
    ppermute x7, waiting for transfers between devices, line_shift(): lax.ppermute(shard, 'y', [(i, (i + by) % devices) for i in range(devices)])  9.9 us
    ppermute x3, starting transfers between devices, core_swap(): return lax.ppermute(shard, 'core', [(0, 1), (1, 0)])  5.76 us
    unnamed x32, local copies, waits for them, and re-layouts  5.52 us
  transfers between devices with their start and end apart: 19, of which 10 were waited for; matrix products, arithmetic and copies ran while one was open for 1% of the time, Pallas kernels for 2%

commit v1 on v0

--- a/solution.py
+++ b/solution.py
@@ -1,5 +1,3 @@
-import functools
-
 import jax
 import jax.numpy as jnp
 import numpy as np
@@ -125,7 +123,7 @@
 
 
 def project_kernel(
-    sides, place_ref, got_ref, own_ref, other_ref, cosine_ref, sine_ref,
+    place_ref, got_ref, own_ref, other_ref, cosine_ref, sine_ref,
     keys_ref, mine_ref, theirs_ref, mine_turned, theirs_turned,
 ):
     bf16, f32 = jnp.bfloat16, jnp.float32
@@ -134,14 +132,13 @@
     _, into, _ = arrivals(got_ref, rows)
     done = jnp.dot(into, got_ref[:, : 2 * count * HEAD_DIM], preferred_element_type=f32)
     is_first = jnp.broadcast_to(place_ref[0], (rows, HEAD_DIM)) == 0
-    own_tiles, other_tiles = [], []
     for i in range(count):
         even = done[:, 2 * i * HEAD_DIM : (2 * i + 1) * HEAD_DIM]
         odd = done[:, (2 * i + 1) * HEAD_DIM : (2 * i + 2) * HEAD_DIM]
         own = jnp.where(is_first, even, odd).astype(bf16)
         other = jnp.where(is_first, odd, even).astype(bf16)
-        own_tiles.append(own)
-        other_tiles.append(other)
+        mine_ref[:, i * HEAD_DIM : (i + 1) * HEAD_DIM] = own
+        theirs_ref[:, i * HEAD_DIM : (i + 1) * HEAD_DIM] = other
         turned = lax.rem(place_ref[1] - i + count, count)
         lanes = pl.ds(pl.multiple_of(turned * HEAD_DIM, HEAD_DIM), HEAD_DIM)
         mine_turned[:, lanes] = own
@@ -154,17 +151,6 @@
         keys_ref[:, h * HEAD_DIM : (h + 1) * HEAD_DIM] = (
             head * cosine_ref[...] + swapped * sine_ref[...]
         ).astype(bf16)
-    source = lax.broadcasted_iota(jnp.int32, (HEAD_DIM, HEAD_DIM), 0)
-    target = lax.broadcasted_iota(jnp.int32, (HEAD_DIM, HEAD_DIM), 1)
-    part = HEAD_DIM // sides
-    wanted = (target % part) // 4 * (4 * sides) + target // part * 4 + target % 4
-    order = jnp.where(source == wanted, 1.0, 0.0).astype(bf16)
-    for tiles, ref in ((own_tiles, mine_ref), (other_tiles, theirs_ref)):
-        moved = jnp.dot(
-            jnp.concatenate(tiles, axis=0), order, preferred_element_type=f32
-        ).astype(bf16)
-        for i in range(count):
-            ref[:, i * HEAD_DIM : (i + 1) * HEAD_DIM] = moved[i * rows : (i + 1) * rows]
 
 
 def rest_kernel(got_ref, queries_ref, values_ref):
@@ -342,11 +328,11 @@
     )(row_target.reshape(1, rows), hidden, queries, values)
 
 
-def project(got, place_of, own_half, other_half, cosine, sine, sides):
+def project(got, place_of, own_half, other_half, cosine, sine):
     rows, (width, kv_width) = cosine.shape[0], own_half.shape
     struct = jax.ShapeDtypeStruct
     return pl.pallas_call(
-        functools.partial(project_kernel, sides),
+        project_kernel,
         out_shape=[struct((rows, w), jnp.bfloat16) for w in (kv_width, width, width)],
         in_specs=[pl.BlockSpec(memory_space=pltpu.SMEM)] + whole(5),
         out_specs=whole(3),
@@ -400,16 +386,13 @@
         other_half,
         jnp.concatenate([cosine[:, 0], cosine[:, 0]], axis=1),
         jnp.concatenate([-sine[:, 0], sine[:, 0]], axis=1),
-        lax.axis_size(ACROSS),
     )
     queries_seq, values_seq = unpack_rest(got, local_rows, width, kv_width)
 
     starts = dialogue_starts(dialogue_lengths[0], positions)
-    near_keys = [seq_shift(keys_seq, by) for by in range(1, SPAN + 1)]
-    values_late, *near_keys = lax.optimization_barrier((values_seq, *near_keys))
-    values_all = [values_seq]
+    near_keys = []
     for by in range(1, SPAN + 1):
-        values_all.append(seq_shift(values_late, by))
+        near_keys.append(seq_shift(keys_seq, by))
     own_grad, grad_1, grad_2, token_loss, weights = attend(
         starts - seq_index * local_rows,
         queries_seq,
@@ -430,13 +413,14 @@
         return jnp.einsum("td,tc->dc", columns, grads, preferred_element_type=f32)
 
     summed = (term(mine, key_grad) + term(partner, core_swap(key_grad))).astype(bf16)
-    sides = lax.axis_size(ACROSS)
-    pieces = jnp.transpose(summed.reshape(lines, sides, -1, kv_width), (1, 0, 2, 3))
-    pieces = pieces.reshape(sides, -1, kv_width)
-    line = jnp.sum(exchange(pieces, ACROSS).astype(f32), axis=0).astype(bf16)
+    values_late, pieces = lax.optimization_barrier(
+        (values_seq, summed.reshape(lines * lax.axis_size("z"), -1, kv_width))
+    )
+    line = jnp.sum(exchange(pieces, ("y", "z")).astype(f32), axis=0)
+    values_all = [values_seq] + [seq_shift(values_late, by) for by in range(1, SPAN + 1)]
     attn_out = attend_output(weights, values_all)
-    last = exchange(line.reshape(-1, 4, kv_width), ("y", "z"))
-    weight_grad = jnp.sum(last.astype(f32), axis=0) * inverse_root
+    last = exchange(line.reshape(lax.axis_size(ACROSS), -1, kv_width), ACROSS)
+    weight_grad = jnp.sum(last, axis=0) * inverse_root
     return (attn_out, token_loss.reshape(local_rows), weight_grad)
 
 

time: 160 us -> 168 us (1.050)
  the two profiles are of different devices: /device:TPU:66 before, /device:TPU:16 now
where the time goes in v1:
time: 168 us; the launch traced here: 167 us
  starting transfers between devices  90.9 us (54%)
  waiting for transfers between devices  53.2 us (32%)
  Pallas kernels  9.75 us (6%)
  local copies, waits for them, and re-layouts  7.74 us (5%)
  other arithmetic  2.17 us (1%)
  matrix products  1.92 us (1%)
    all_to_all x4, starting transfers between devices, exchange(): return lax.all_to_all(pieces, axes, split_axis=0, concat_axis=0, tiled=True)  37.3 us
    all_to_all x4, waiting for transfers between devices, exchange(): return lax.all_to_all(pieces, axes, split_axis=0, concat_axis=0, tiled=True)  29.6 us
    ppermute x7, starting transfers between devices, line_shift(): lax.ppermute(shard, 'y', [(i, (i + by) % devices) for i in range(devices)])  27.4 us
    ppermute x6, starting transfers between devices, seq_shift(): return lax.ppermute(shard, SEQ, pairs)  20.4 us
    ppermute x7, waiting for transfers between devices, line_shift(): lax.ppermute(shard, 'y', [(i, (i + by) % devices) for i in range(devices)])  12.5 us
    ppermute x6, waiting for transfers between devices, seq_shift(): return lax.ppermute(shard, SEQ, pairs)  8.57 us
    ppermute x3, starting transfers between devices, core_swap(): return lax.ppermute(shard, 'core', [(0, 1), (1, 0)])  5.76 us
    unnamed x32, local copies, waits for them, and re-layouts  5.51 us
  transfers between devices with their start and end apart: 20, of which 12 were waited for; matrix products, arithmetic and copies ran while one was open for 1% of the time, Pallas kernels for 2%

profile of v1, /device:TPU:16, one launch (start us, length us, event | category | flops | bytes accessed | tf_op | source)
XLA Modules:
  0.0 166.8 jit_solution(4481157155877010973)
XLA Ops:
  0.6 1.4 broadcast_in_dim.26
  2.0 13.2 %all-to-all-start.1 = ((bf16[32,4,512]{2,1,0:T(4,128)(2,1)}), bf16[32,4,512]{2,1,0:T(4,128)(2,1)S(1)}, u32[]{:S(2)}, u32[]{:S(2)}) async-start(bf16[32,4,512]{2,1,0:T(4,128)(2,1)} %broadcast_in_dim.26), calls=%async_computation.1 | async-start | bytes 262144 | tf_op jit(solution)/shard_map/all_to_all | solution.py:26
  15.2 1.0 copy-done.1
  16.2 1.0 copy-done.2
  17.3 0.9 copy-done.3
  18.2 0.7 copy-done.6
  18.8 0.8 pack_rows.1
  19.7 1.2 copy-done
  20.9 4.7 %all-to-all-done.1 = bf16[32,4,512]{2,1,0:T(4,128)(2,1)S(1)} async-done(((bf16[32,4,512]{2,1,0:T(4,128)(2,1)}), bf16[32,4,512]{2,1,0:T(4,128)(2,1)S(1)}, u32[]{:S(2)}, u32[]{:S(2)}) %all-to-all-start.1) | async-done | bytes 131104 | tf_op jit(solution)/shard_map/all_to_all | solution.py:26
  25.6 5.1 %all-to-all-start = ((bf16[32,8,3584]{2,1,0:T(8,128)(2,1)}), bf16[32,8,3584]{2,1,0:T(8,128)(2,1)S(1)}, u32[]{:S(2)}, u32[]{:S(2)}) async-start(bf16[32,8,3584]{2,1,0:T(8,128)(2,1)} %bitcast.21), calls=%async_computation | async-start | bytes 3670016 | tf_op jit(solution)/shard_map/all_to_all | solution.py:26
  30.7 3.5 %collective-permute-start = (bf16[128,512]{1,0:T(8,128)(2,1)S(1)}, bf16[128,512]{1,0:T(8,128)(2,1)S(1)}, u32[]{:S(2)}, u32[]{:S(2)}) collective-permute-start(bf16[128,512]{1,0:T(8,128)(2,1)S(1)} %reshape.132), channel_id=1, source_target_pairs={{0,64},{64,128},{128,192},{192,256},{256,320},{320,384},{384,448},... | collective-permute-start | bytes 393224 | tf_op jit(solution)/shard_map/ppermute | solution.py:37
  34.2 4.8 %collective-permute-start.1 = (bf16[128,512]{1,0:T(8,128)(2,1)S(1)}, bf16[128,512]{1,0:T(8,128)(2,1)S(1)}, u32[]{:S(2)}, u32[]{:S(2)}) collective-permute-start(bf16[128,512]{1,0:T(8,128)(2,1)S(1)} %reshape.132), channel_id=1, source_target_pairs={{0,128},{64,192},{128,256},{192,320},{256,384},{320,448},{384,0},{... | collective-permute-start | bytes 393224 | tf_op jit(solution)/shard_map/ppermute | solution.py:37
  39.1 2.1 %collective-permute-start.2 = (bf16[128,512]{1,0:T(8,128)(2,1)S(1)}, bf16[128,512]{1,0:T(8,128)(2,1)S(1)}, u32[]{:S(2)}, u32[]{:S(2)}) collective-permute-start(bf16[128,512]{1,0:T(8,128)(2,1)S(1)} %reshape.132), channel_id=1, source_target_pairs={{0,192},{64,256},{128,320},{192,384},{256,448},{320,0},{384,64},{4... | collective-permute-start | bytes 393224 | tf_op jit(solution)/shard_map/ppermute | solution.py:37
  41.2 7.5 %collective-permute-start.3 = (bf16[128,512]{1,0:T(8,128)(2,1)S(1)}, bf16[128,512]{1,0:T(8,128)(2,1)S(1)}, u32[]{:S(2)}, u32[]{:S(2)}) collective-permute-start(bf16[128,512]{1,0:T(8,128)(2,1)S(1)} %reshape.132), channel_id=1, source_target_pairs={{0,256},{64,320},{128,384},{192,448},{256,0},{320,64},{384,128},{4... | collective-permute-start | bytes 393224 | tf_op jit(solution)/shard_map/ppermute | solution.py:37
  48.7 2.1 %collective-permute-start.4 = (bf16[128,512]{1,0:T(8,128)(2,1)S(1)}, bf16[128,512]{1,0:T(8,128)(2,1)S(1)}, u32[]{:S(2)}, u32[]{:S(2)}) collective-permute-start(bf16[128,512]{1,0:T(8,128)(2,1)S(1)} %reshape.132), channel_id=1, source_target_pairs={{0,320},{64,384},{128,448},{192,0},{256,64},{320,128},{384,192},{4... | collective-permute-start | bytes 393224 | tf_op jit(solution)/shard_map/ppermute | solution.py:37
  50.9 4.1 %collective-permute-start.5 = (bf16[128,512]{1,0:T(8,128)(2,1)S(1)}, bf16[128,512]{1,0:T(8,128)(2,1)S(1)}, u32[]{:S(2)}, u32[]{:S(2)}) collective-permute-start(bf16[128,512]{1,0:T(8,128)(2,1)S(1)} %reshape.132), channel_id=1, source_target_pairs={{0,384},{64,448},{128,0},{192,64},{256,128},{320,192},{384,256},{4... | collective-permute-start | bytes 393224 | tf_op jit(solution)/shard_map/ppermute | solution.py:37
  55.0 3.3 %collective-permute-start.6 = (bf16[128,512]{1,0:T(8,128)(2,1)S(1)}, bf16[128,512]{1,0:T(8,128)(2,1)S(1)}, u32[]{:S(2)}, u32[]{:S(2)}) collective-permute-start(bf16[128,512]{1,0:T(8,128)(2,1)S(1)} %reshape.132), channel_id=1, source_target_pairs={{0,448},{64,0},{128,64},{192,128},{256,192},{320,256},{384,320},{4... | collective-permute-start | bytes 393224 | tf_op jit(solution)/shard_map/ppermute | solution.py:37
  58.3 2.2 %collective-permute-done.3 = bf16[128,512]{1,0:T(8,128)(2,1)S(1)} collective-permute-done((bf16[128,512]{1,0:T(8,128)(2,1)S(1)}, bf16[128,512]{1,0:T(8,128)(2,1)S(1)}, u32[]{:S(2)}, u32[]{:S(2)}) %collective-permute-start.3) | collective-permute-done | bytes 131104 | tf_op jit(solution)/shard_map/ppermute | solution.py:37
  60.5 2.3 %collective-permute-done.4 = bf16[128,512]{1,0:T(8,128)(2,1)S(1)} collective-permute-done((bf16[128,512]{1,0:T(8,128)(2,1)S(1)}, bf16[128,512]{1,0:T(8,128)(2,1)S(1)}, u32[]{:S(2)}, u32[]{:S(2)}) %collective-permute-start.4) | collective-permute-done | bytes 131104 | tf_op jit(solution)/shard_map/ppermute | solution.py:37
  62.8 6.4 %collective-permute-done.5 = bf16[128,512]{1,0:T(8,128)(2,1)S(1)} collective-permute-done((bf16[128,512]{1,0:T(8,128)(2,1)S(1)}, bf16[128,512]{1,0:T(8,128)(2,1)S(1)}, u32[]{:S(2)}, u32[]{:S(2)}) %collective-permute-start.5) | collective-permute-done | bytes 131104 | tf_op jit(solution)/shard_map/ppermute | solution.py:37
  69.2 1.7 collective-permute-done.6
  70.8 1.9 %collective-permute-start.7 = (bf16[1024,512]{1,0:T(8,128)(2,1)S(1)}, bf16[1024,512]{1,0:T(8,128)(2,1)}, u32[]{:S(2)}, u32[]{:S(2)}) collective-permute-start(bf16[1024,512]{1,0:T(8,128)(2,1)S(1)} %constant_dynamic-update-slice_fusion.own_ref), channel_id=1, source_target_pairs={{0,32},{32,0},{1,33},{33,1},{2,34},{34,2},{3,35},{35,3},{4,36},{36... | collective-permute-start | bytes 3145736 | tf_op jit(solution)/shard_map/ppermute | solution.py:41
  73.6 0.5 copy-done.9
  74.3 1.2 collective-permute-done.7.other_ref
  75.6 2.2 %project.1 = (bf16[128,512]{1,0:T(8,128)(2,1)S(1)}, bf16[128,1024]{1,0:T(8,128)(2,1)S(1)}, bf16[128,1024]{1,0:T(8,128)(2,1)S(1)}) custom-call(s32[2]{0:T(128)S(1)} %pad_add_fusion.place_ref, bf16[256,3584]{1,0:T(8,128)(2,1)S(1)} %bitcast.19, bf16[1024,512]{1,0:T(8,128)(2,1)S(1)} %constant_dynamic-update-slice_fusion.own_ref, ...), custom_call_target="tpu_custom_call" | custom-call | tf_op jit(solution)/shard_map/project/pallas_call | solution.py:334
  77.8 3.4 %collective-permute-start.8 = (bf16[128,512]{1,0:T(8,128)(2,1)S(1)}, bf16[128,512]{1,0:T(8,128)(2,1)S(1)}, u32[]{:S(2)}, u32[]{:S(2)}) collective-permute-start(bf16[128,512]{1,0:T(8,128)(2,1)S(1)} %get-tuple-element.18.k0_ref), channel_id=1, source_target_pairs={{0,1},{1,2},{2,3},{3,4},{4,5},{5,6},{6,7},{7,8},{8,9},{9,10},{10,1... | collective-permute-start | bytes 393224 | tf_op jit(solution)/shard_map/ppermute | solution.py:32
  81.2 4.6 %collective-permute-start.9 = (bf16[128,512]{1,0:T(8,128)(2,1)S(1)}, bf16[128,512]{1,0:T(8,128)(2,1)S(1)}, u32[]{:S(2)}, u32[]{:S(2)}) collective-permute-start(bf16[128,512]{1,0:T(8,128)(2,1)S(1)} %get-tuple-element.18.k0_ref), channel_id=1, source_target_pairs={{0,2},{1,3},{2,4},{3,5},{4,6},{5,7},{6,8},{7,9},{8,10},{9,11},{10,... | collective-permute-start | bytes 393224 | tf_op jit(solution)/shard_map/ppermute | solution.py:32
  85.8 0.6 unpack_rest.1
  86.4 2.1 %collective-permute-done.9.k2_ref = bf16[128,512]{1,0:T(8,128)(2,1)S(1)} collective-permute-done((bf16[128,512]{1,0:T(8,128)(2,1)S(1)}, bf16[128,512]{1,0:T(8,128)(2,1)S(1)}, u32[]{:S(2)}, u32[]{:S(2)}) %collective-permute-start.9) | collective-permute-done | bytes 131104 | tf_op jit(solution)/shard_map/ppermute | solution.py:32
  88.5 4.8 %attend.1 = (f32[128,512]{1,0:T(8,128)S(1)}, bf16[128,512]{1,0:T(8,128)(2,1)S(1)}, bf16[128,512]{1,0:T(8,128)(2,1)S(1)}, f32[1,128]{1,0:T(1,128)}, bf16[4,384,512]{2,1,0:T(8,128)(2,1)S(1)}) custom-call(s32[1,128]{1,0:T(1,128)S(1)} %subtract_bitcast_fusion.start_ref, bf16[128,2048]{1,0:T(8,128)(2,1)S(1)} %get-tuple-element.17.q_ref, ...), custom_call_target="tpu_custom_call" | custom-call | tf_op jit(solution)/shard_map/attend/pallas_call | solution.py:283
  93.3 1.3 collective-permute-start.11
  94.6 1.3 collective-permute-start.10
  95.9 1.9 %collective-permute-start.12 = (bf16[128,1024]{1,0:T(8,128)(2,1)S(1)}, bf16[128,1024]{1,0:T(8,128)(2,1)S(1)}, u32[]{:S(2)}, u32[]{:S(2)}) collective-permute-start(bf16[128,1024]{1,0:T(8,128)(2,1)S(1)} %get-tuple-element.27), channel_id=1, source_target_pairs={{0,32},{32,0},{1,33},{33,1},{2,34},{34,2},{3,35},{35,3},{4,36},{36... | collective-permute-start | bytes 786440 | tf_op jit(solution)/shard_map/ppermute | solution.py:41
  97.8 4.3 %collective-permute-done.11 = bf16[128,512]{1,0:T(8,128)(2,1)S(1)} collective-permute-done((bf16[128,512]{1,0:T(8,128)(2,1)S(1)}, bf16[128,512]{1,0:T(8,128)(2,1)S(1)}, u32[]{:S(2)}, u32[]{:S(2)}) %collective-permute-start.11) | collective-permute-done | bytes 131104 | tf_op jit(solution)/shard_map/ppermute | solution.py:32
  102.1 2.1 %collective-permute-done.10 = bf16[128,512]{1,0:T(8,128)(2,1)S(1)} collective-permute-done((bf16[128,512]{1,0:T(8,128)(2,1)S(1)}, bf16[128,512]{1,0:T(8,128)(2,1)S(1)}, u32[]{:S(2)}, u32[]{:S(2)}) %collective-permute-start.10) | collective-permute-done | bytes 131104 | tf_op jit(solution)/shard_map/ppermute | solution.py:32
  105.0 1.9 %collective-permute-start.13 = (bf16[128,512]{1,0:T(8,128)(2,1)S(1)}, bf16[128,512]{1,0:T(8,128)(2,1)S(1)}, u32[]{:S(2)}, u32[]{:S(2)}) collective-permute-start(bf16[128,512]{1,0:T(8,128)(2,1)S(1)} %bitcast.25), channel_id=1, source_target_pairs={{0,32},{32,0},{1,33},{33,1},{2,34},{34,2},{3,35},{35,3},{4,36},{36... | collective-permute-start | bytes 393224 | tf_op jit(solution)/shard_map/ppermute | solution.py:41
  106.9 1.3 collective-permute-done.13
  108.2 0.4 fusion.2
  108.6 1.5 add_convert_fusion
  110.1 13.3 %all-to-all-start.2 = ((bf16[64,16,512]{2,1,0:T(8,128)(2,1)}), bf16[64,16,512]{2,1,0:T(8,128)(2,1)S(1)}, u32[]{:S(2)}, u32[]{:S(2)}) async-start(bf16[64,16,512]{2,1,0:T(8,128)(2,1)} %bitcast.8), calls=%async_computation.2 | async-start | bytes 2097152 | tf_op jit(solution)/shard_map/all_to_all | solution.py:26
  123.4 3.5 %collective-permute-start.14 = (bf16[128,512]{1,0:T(8,128)(2,1)S(1)}, bf16[128,512]{1,0:T(8,128)(2,1)S(1)}, u32[]{:S(2)}, u32[]{:S(2)}) collective-permute-start(bf16[128,512]{1,0:T(8,128)(2,1)S(1)} %get-tuple-element.28.v0_ref), channel_id=1, source_target_pairs={{0,1},{1,2},{2,3},{3,4},{4,5},{5,6},{6,7},{7,8},{8,9},{9,10},{10,1... | collective-permute-start | bytes 393224 | tf_op jit(solution)/shard_map/ppermute | solution.py:32
  126.9 6.3 %collective-permute-start.15 = (bf16[128,512]{1,0:T(8,128)(2,1)S(1)}, bf16[128,512]{1,0:T(8,128)(2,1)S(1)}, u32[]{:S(2)}, u32[]{:S(2)}) collective-permute-start(bf16[128,512]{1,0:T(8,128)(2,1)S(1)} %get-tuple-element.28.v0_ref), channel_id=1, source_target_pairs={{0,2},{1,3},{2,4},{3,5},{4,6},{5,7},{6,8},{7,9},{8,10},{9,11},{10,... | collective-permute-start | bytes 393224 | tf_op jit(solution)/shard_map/ppermute | solution.py:32
  133.3 20.8 %all-to-all-done.2 = bf16[64,16,512]{2,1,0:T(8,128)(2,1)S(1)} async-done(((bf16[64,16,512]{2,1,0:T(8,128)(2,1)}), bf16[64,16,512]{2,1,0:T(8,128)(2,1)S(1)}, u32[]{:S(2)}, u32[]{:S(2)}) %all-to-all-start.2) | async-done | bytes 1048608 | tf_op jit(solution)/shard_map/all_to_all | solution.py:26
  154.2 0.6 reshape.136
  154.9 5.8 %all-to-all-start.3 = ((f32[4,4,512]{2,1,0:T(4,128)}), f32[4,4,512]{2,1,0:T(4,128)S(1)}, u32[]{:S(2)}, u32[]{:S(2)}) async-start(f32[4,4,512]{2,1,0:T(4,128)} %reshape.136), calls=%async_computation.3 | async-start | bytes 65536 | tf_op jit(solution)/shard_map/all_to_all | solution.py:26
  160.7 1.4 attend_output.1
  162.1 4.1 %all-to-all-done.3 = f32[4,4,512]{2,1,0:T(4,128)S(1)} async-done(((f32[4,4,512]{2,1,0:T(4,128)}), f32[4,4,512]{2,1,0:T(4,128)S(1)}, u32[]{:S(2)}, u32[]{:S(2)}) %all-to-all-start.3) | async-done | bytes 32800 | tf_op jit(solution)/shard_map/all_to_all | solution.py:26
  166.2 0.6 broadcast_multiply_fusion
  (53 shorter events, 2.0 us)
Async XLA Ops:
  2.0 23.6 %all-to-all-start.1 = ((bf16[32,4,512]{2,1,0:T(4,128)(2,1)}), bf16[32,4,512]{2,1,0:T(4,128)(2,1)S(1)}, u32[]{:S(2)}, u32[]{:S(2)}) async-start(bf16[32,4,512]{2,1,0:T(4,128)(2,1)} %broadcast_in_dim.26), calls=%async_computation.1 | async-start | bytes 262144 | tf_op jit(solution)/shard_map/all_to_all | solution.py:26
  15.2 1.0 copy-start.1
  16.2 1.0 copy-start.2
  17.3 0.9 copy-start.3
  18.2 0.7 copy-start.6
  19.7 1.3 copy-start
  25.6 49.9 %all-to-all-start = ((bf16[32,8,3584]{2,1,0:T(8,128)(2,1)}), bf16[32,8,3584]{2,1,0:T(8,128)(2,1)S(1)}, u32[]{:S(2)}, u32[]{:S(2)}) async-start(bf16[32,8,3584]{2,1,0:T(8,128)(2,1)} %bitcast.21), calls=%async_computation | async-start | bytes 3670016 | tf_op jit(solution)/shard_map/all_to_all | solution.py:26
  30.7 42.1 %copy-start.11 = (s32[1,64]{1,0:T(1,128)S(1)}, s32[1,64]{1,0:T(1,128)}, u32[]{:S(2)}) copy-start(s32[1,64]{1,0:T(1,128)} %param.13) | copy-start | bytes 772
  30.7 20.1 %collective-permute-start = (bf16[128,512]{1,0:T(8,128)(2,1)S(1)}, bf16[128,512]{1,0:T(8,128)(2,1)S(1)}, u32[]{:S(2)}, u32[]{:S(2)}) collective-permute-start(bf16[128,512]{1,0:T(8,128)(2,1)S(1)} %reshape.132), channel_id=1, source_target_pairs={{0,64},{64,128},{128,192},{192,256},{256,320},{320,384},{384,448},... | collective-permute-start | bytes 393224 | tf_op jit(solution)/shard_map/ppermute | solution.py:37
  34.2 20.7 %collective-permute-start.1 = (bf16[128,512]{1,0:T(8,128)(2,1)S(1)}, bf16[128,512]{1,0:T(8,128)(2,1)S(1)}, u32[]{:S(2)}, u32[]{:S(2)}) collective-permute-start(bf16[128,512]{1,0:T(8,128)(2,1)S(1)} %reshape.132), channel_id=1, source_target_pairs={{0,128},{64,192},{128,256},{192,320},{256,384},{320,448},{384,0},{... | collective-permute-start | bytes 393224 | tf_op jit(solution)/shard_map/ppermute | solution.py:37
  39.1 19.2 %collective-permute-start.2 = (bf16[128,512]{1,0:T(8,128)(2,1)S(1)}, bf16[128,512]{1,0:T(8,128)(2,1)S(1)}, u32[]{:S(2)}, u32[]{:S(2)}) collective-permute-start(bf16[128,512]{1,0:T(8,128)(2,1)S(1)} %reshape.132), channel_id=1, source_target_pairs={{0,192},{64,256},{128,320},{192,384},{256,448},{320,0},{384,64},{4... | collective-permute-start | bytes 393224 | tf_op jit(solution)/shard_map/ppermute | solution.py:37
  41.2 19.2 %collective-permute-start.3 = (bf16[128,512]{1,0:T(8,128)(2,1)S(1)}, bf16[128,512]{1,0:T(8,128)(2,1)S(1)}, u32[]{:S(2)}, u32[]{:S(2)}) collective-permute-start(bf16[128,512]{1,0:T(8,128)(2,1)S(1)} %reshape.132), channel_id=1, source_target_pairs={{0,256},{64,320},{128,384},{192,448},{256,0},{320,64},{384,128},{4... | collective-permute-start | bytes 393224 | tf_op jit(solution)/shard_map/ppermute | solution.py:37
  48.7 14.0 %collective-permute-start.4 = (bf16[128,512]{1,0:T(8,128)(2,1)S(1)}, bf16[128,512]{1,0:T(8,128)(2,1)S(1)}, u32[]{:S(2)}, u32[]{:S(2)}) collective-permute-start(bf16[128,512]{1,0:T(8,128)(2,1)S(1)} %reshape.132), channel_id=1, source_target_pairs={{0,320},{64,384},{128,448},{192,0},{256,64},{320,128},{384,192},{4... | collective-permute-start | bytes 393224 | tf_op jit(solution)/shard_map/ppermute | solution.py:37
  50.9 18.3 %collective-permute-start.5 = (bf16[128,512]{1,0:T(8,128)(2,1)S(1)}, bf16[128,512]{1,0:T(8,128)(2,1)S(1)}, u32[]{:S(2)}, u32[]{:S(2)}) collective-permute-start(bf16[128,512]{1,0:T(8,128)(2,1)S(1)} %reshape.132), channel_id=1, source_target_pairs={{0,384},{64,448},{128,0},{192,64},{256,128},{320,192},{384,256},{4... | collective-permute-start | bytes 393224 | tf_op jit(solution)/shard_map/ppermute | solution.py:37
  55.0 15.9 %collective-permute-start.6 = (bf16[128,512]{1,0:T(8,128)(2,1)S(1)}, bf16[128,512]{1,0:T(8,128)(2,1)S(1)}, u32[]{:S(2)}, u32[]{:S(2)}) collective-permute-start(bf16[128,512]{1,0:T(8,128)(2,1)S(1)} %reshape.132), channel_id=1, source_target_pairs={{0,448},{64,0},{128,64},{192,128},{256,192},{320,256},{384,320},{4... | collective-permute-start | bytes 393224 | tf_op jit(solution)/shard_map/ppermute | solution.py:37
  70.8 4.7 %collective-permute-start.7 = (bf16[1024,512]{1,0:T(8,128)(2,1)S(1)}, bf16[1024,512]{1,0:T(8,128)(2,1)}, u32[]{:S(2)}, u32[]{:S(2)}) collective-permute-start(bf16[1024,512]{1,0:T(8,128)(2,1)S(1)} %constant_dynamic-update-slice_fusion.own_ref), channel_id=1, source_target_pairs={{0,32},{32,0},{1,33},{33,1},{2,34},{34,2},{3,35},{35,3},{4,36},{36... | collective-permute-start | bytes 3145736 | tf_op jit(solution)/shard_map/ppermute | solution.py:41
  73.5 0.6 copy-start.9
  73.5 2.0 %copy-start.7 = (f32[128,64]{1,0:T(8,128)}, f32[128,64]{1,0:T(8,128)S(1)}, u32[]{:S(2)}) copy-start(f32[128,64]{1,0:T(8,128)S(1)} %get-tuple-element.33) | copy-start | bytes 98308
  75.5 13.0 %copy-start.4 = (s32[128,128]{1,0:T(8,128)S(1)}, s32[128,128]{1,0:T(8,128)}, u32[]{:S(2)}) copy-start(s32[128,128]{1,0:T(8,128)} %pick_ref.1) | copy-start | bytes 196612
  75.5 13.0 %copy-start.5 = (f32[128,128]{1,0:T(8,128)S(1)}, f32[128,128]{1,0:T(8,128)}, u32[]{:S(2)}) copy-start(f32[128,128]{1,0:T(8,128)} %prob_ref.1) | copy-start | bytes 196612
  77.8 8.6 %collective-permute-start.8 = (bf16[128,512]{1,0:T(8,128)(2,1)S(1)}, bf16[128,512]{1,0:T(8,128)(2,1)S(1)}, u32[]{:S(2)}, u32[]{:S(2)}) collective-permute-start(bf16[128,512]{1,0:T(8,128)(2,1)S(1)} %get-tuple-element.18.k0_ref), channel_id=1, source_target_pairs={{0,1},{1,2},{2,3},{3,4},{4,5},{5,6},{6,7},{7,8},{8,9},{9,10},{10,1... | collective-permute-start | bytes 393224 | tf_op jit(solution)/shard_map/ppermute | solution.py:32
  81.2 7.3 %collective-permute-start.9 = (bf16[128,512]{1,0:T(8,128)(2,1)S(1)}, bf16[128,512]{1,0:T(8,128)(2,1)S(1)}, u32[]{:S(2)}, u32[]{:S(2)}) collective-permute-start(bf16[128,512]{1,0:T(8,128)(2,1)S(1)} %get-tuple-element.18.k0_ref), channel_id=1, source_target_pairs={{0,2},{1,3},{2,4},{3,5},{4,6},{5,7},{6,8},{7,9},{8,10},{9,11},{10,... | collective-permute-start | bytes 393224 | tf_op jit(solution)/shard_map/ppermute | solution.py:32
  85.8 18.6 %copy-start.8 = (f32[128,64]{1,0:T(8,128)S(1)}, f32[128,64]{1,0:T(8,128)}, u32[]{:S(2)}) copy-start(f32[128,64]{1,0:T(8,128)} %copy-done.7) | copy-start | bytes 98308
  85.8 18.6 %copy-start.10 = (f32[128,64]{1,0:T(8,128)S(1)}, f32[128,64]{1,0:T(8,128)}, u32[]{:S(2)}) copy-start(f32[128,64]{1,0:T(8,128)} %copy-done.9) | copy-start | bytes 98308
  93.3 8.8 %collective-permute-start.11 = (bf16[128,512]{1,0:T(8,128)(2,1)S(1)}, bf16[128,512]{1,0:T(8,128)(2,1)S(1)}, u32[]{:S(2)}, u32[]{:S(2)}) collective-permute-start(bf16[128,512]{1,0:T(8,128)(2,1)S(1)} %get-tuple-element.26), channel_id=1, source_target_pairs={{2,0},{3,1},{4,2},{5,3},{6,4},{7,5},{8,6},{9,7},{10,8},{11,9},{12,... | collective-permute-start | bytes 393224 | tf_op jit(solution)/shard_map/ppermute | solution.py:32
  94.6 9.7 %collective-permute-start.10 = (bf16[128,512]{1,0:T(8,128)(2,1)S(1)}, bf16[128,512]{1,0:T(8,128)(2,1)S(1)}, u32[]{:S(2)}, u32[]{:S(2)}) collective-permute-start(bf16[128,512]{1,0:T(8,128)(2,1)S(1)} %get-tuple-element.25), channel_id=1, source_target_pairs={{1,0},{2,1},{3,2},{4,3},{5,4},{6,5},{7,6},{8,7},{9,8},{10,9},{11,1... | collective-permute-start | bytes 393224 | tf_op jit(solution)/shard_map/ppermute | solution.py:32
  95.9 11.0 %collective-permute-start.12 = (bf16[128,1024]{1,0:T(8,128)(2,1)S(1)}, bf16[128,1024]{1,0:T(8,128)(2,1)S(1)}, u32[]{:S(2)}, u32[]{:S(2)}) collective-permute-start(bf16[128,1024]{1,0:T(8,128)(2,1)S(1)} %get-tuple-element.27), channel_id=1, source_target_pairs={{0,32},{32,0},{1,33},{33,1},{2,34},{34,2},{3,35},{35,3},{4,36},{36... | collective-permute-start | bytes 786440 | tf_op jit(solution)/shard_map/ppermute | solution.py:41
  105.0 3.2 %collective-permute-start.13 = (bf16[128,512]{1,0:T(8,128)(2,1)S(1)}, bf16[128,512]{1,0:T(8,128)(2,1)S(1)}, u32[]{:S(2)}, u32[]{:S(2)}) collective-permute-start(bf16[128,512]{1,0:T(8,128)(2,1)S(1)} %bitcast.25), channel_id=1, source_target_pairs={{0,32},{32,0},{1,33},{33,1},{2,34},{34,2},{3,35},{35,3},{4,36},{36... | collective-permute-start | bytes 393224 | tf_op jit(solution)/shard_map/ppermute | solution.py:41
  110.1 43.9 %all-to-all-start.2 = ((bf16[64,16,512]{2,1,0:T(8,128)(2,1)}), bf16[64,16,512]{2,1,0:T(8,128)(2,1)S(1)}, u32[]{:S(2)}, u32[]{:S(2)}) async-start(bf16[64,16,512]{2,1,0:T(8,128)(2,1)} %bitcast.8), calls=%async_computation.2 | async-start | bytes 2097152 | tf_op jit(solution)/shard_map/all_to_all | solution.py:26
  123.4 37.3 %collective-permute-start.14 = (bf16[128,512]{1,0:T(8,128)(2,1)S(1)}, bf16[128,512]{1,0:T(8,128)(2,1)S(1)}, u32[]{:S(2)}, u32[]{:S(2)}) collective-permute-start(bf16[128,512]{1,0:T(8,128)(2,1)S(1)} %get-tuple-element.28.v0_ref), channel_id=1, source_target_pairs={{0,1},{1,2},{2,3},{3,4},{4,5},{5,6},{6,7},{7,8},{8,9},{9,10},{10,1... | collective-permute-start | bytes 393224 | tf_op jit(solution)/shard_map/ppermute | solution.py:32
  126.9 33.8 %collective-permute-start.15 = (bf16[128,512]{1,0:T(8,128)(2,1)S(1)}, bf16[128,512]{1,0:T(8,128)(2,1)S(1)}, u32[]{:S(2)}, u32[]{:S(2)}) collective-permute-start(bf16[128,512]{1,0:T(8,128)(2,1)S(1)} %get-tuple-element.28.v0_ref), channel_id=1, source_target_pairs={{0,2},{1,3},{2,4},{3,5},{4,6},{5,7},{6,8},{7,9},{8,10},{9,11},{10,... | collective-permute-start | bytes 393224 | tf_op jit(solution)/shard_map/ppermute | solution.py:32
  154.9 11.3 %all-to-all-start.3 = ((f32[4,4,512]{2,1,0:T(4,128)}), f32[4,4,512]{2,1,0:T(4,128)S(1)}, u32[]{:S(2)}, u32[]{:S(2)}) async-start(f32[4,4,512]{2,1,0:T(4,128)} %reshape.136), calls=%async_computation.3 | async-start | bytes 65536 | tf_op jit(solution)/shard_map/all_to_all | solution.py:26

commit v2 on v0

--- a/solution.py
+++ b/solution.py
@@ -405,11 +405,9 @@
     queries_seq, values_seq = unpack_rest(got, local_rows, width, kv_width)
 
     starts = dialogue_starts(dialogue_lengths[0], positions)
-    near_keys = [seq_shift(keys_seq, by) for by in range(1, SPAN + 1)]
-    values_late, *near_keys = lax.optimization_barrier((values_seq, *near_keys))
-    values_all = [values_seq]
+    near_keys = []
     for by in range(1, SPAN + 1):
-        values_all.append(seq_shift(values_late, by))
+        near_keys.append(seq_shift(keys_seq, by))
     own_grad, grad_1, grad_2, token_loss, weights = attend(
         starts - seq_index * local_rows,
         queries_seq,
@@ -432,8 +430,13 @@
     summed = (term(mine, key_grad) + term(partner, core_swap(key_grad))).astype(bf16)
     sides = lax.axis_size(ACROSS)
     pieces = jnp.transpose(summed.reshape(lines, sides, -1, kv_width), (1, 0, 2, 3))
-    pieces = pieces.reshape(sides, -1, kv_width)
+    values_late, pieces = lax.optimization_barrier(
+        (values_seq, pieces.reshape(sides, -1, kv_width))
+    )
     line = jnp.sum(exchange(pieces, ACROSS).astype(f32), axis=0).astype(bf16)
+    values_all = [values_seq]
+    for by in range(1, SPAN + 1):
+        values_all.append(seq_shift(values_late, by))
     attn_out = attend_output(weights, values_all)
     last = exchange(line.reshape(-1, 4, kv_width), ("y", "z"))
     weight_grad = jnp.sum(last.astype(f32), axis=0) * inverse_root

time: 160 us -> 160 us (level)
  no operation moved by 1% of the time
where the time goes in v2:
time: 160 us
  starting transfers between devices  88.3 us (55%)
  waiting for transfers between devices  29.1 us (18%)
  blocking collectives  20 us (12%)
  Pallas kernels  9.76 us (6%)
  local copies, waits for them, and re-layouts  8.01 us (5%)
  other arithmetic  2.29 us (1%)
    all_to_all x3, starting transfers between devices, exchange(): return lax.all_to_all(pieces, axes, split_axis=0, concat_axis=0, tiled=True)  30.4 us
    ppermute x7, starting transfers between devices, line_shift(): lax.ppermute(shard, 'y', [(i, (i + by) % devices) for i in range(devices)])  30.4 us
    ppermute x6, starting transfers between devices, seq_shift(): return lax.ppermute(shard, SEQ, pairs)  21.7 us
    all_to_all x1, blocking collectives, exchange(): return lax.all_to_all(pieces, axes, split_axis=0, concat_axis=0, tiled=True)  20 us
    ppermute x6, waiting for transfers between devices, seq_shift(): return lax.ppermute(shard, SEQ, pairs)  13.7 us
    ppermute x7, waiting for transfers between devices, line_shift(): lax.ppermute(shard, 'y', [(i, (i + by) % devices) for i in range(devices)])  9.9 us
    ppermute x3, starting transfers between devices, core_swap(): return lax.ppermute(shard, 'core', [(0, 1), (1, 0)])  5.76 us
    unnamed x32, local copies, waits for them, and re-layouts  5.52 us
  transfers between devices with their start and end apart: 19, of which 10 were waited for; matrix products, arithmetic and copies ran while one was open for 1% of the time, Pallas kernels for 2%

profile of v2, /device:TPU:66, one launch (start us, length us, event | category | flops | bytes accessed | tf_op | source)
XLA Modules:
  0.0 159.5 jit_solution(16680232769146778725)
XLA Ops:
  0.6 1.4 broadcast_in_dim.26
  2.0 12.6 %all-to-all-start.1 = ((bf16[32,4,512]{2,1,0:T(4,128)(2,1)}), bf16[32,4,512]{2,1,0:T(4,128)(2,1)S(1)}, u32[]{:S(2)}, u32[]{:S(2)}) async-start(bf16[32,4,512]{2,1,0:T(4,128)(2,1)} %broadcast_in_dim.26), calls=%async_computation.1 | async-start | bytes 262144 | tf_op jit(solution)/shard_map/all_to_all | solution.py:28
  14.6 1.0 copy-done.1
  15.6 1.0 copy-done.2
  16.7 0.9 copy-done.3
  17.6 0.7 copy-done.6
  18.2 0.8 pack_rows.1
  19.1 1.3 copy-done
  20.3 3.0 %all-to-all-done.1 = bf16[32,4,512]{2,1,0:T(4,128)(2,1)S(1)} async-done(((bf16[32,4,512]{2,1,0:T(4,128)(2,1)}), bf16[32,4,512]{2,1,0:T(4,128)(2,1)S(1)}, u32[]{:S(2)}, u32[]{:S(2)}) %all-to-all-start.1) | async-done | bytes 131104 | tf_op jit(solution)/shard_map/all_to_all | solution.py:28
  23.3 6.8 %all-to-all-start = ((bf16[32,8,3584]{2,1,0:T(8,128)(2,1)}), bf16[32,8,3584]{2,1,0:T(8,128)(2,1)S(1)}, u32[]{:S(2)}, u32[]{:S(2)}) async-start(bf16[32,8,3584]{2,1,0:T(8,128)(2,1)} %bitcast.24), calls=%async_computation | async-start | bytes 3670016 | tf_op jit(solution)/shard_map/all_to_all | solution.py:28
  30.2 3.5 %collective-permute-start = (bf16[128,512]{1,0:T(8,128)(2,1)S(1)}, bf16[128,512]{1,0:T(8,128)(2,1)S(1)}, u32[]{:S(2)}, u32[]{:S(2)}) collective-permute-start(bf16[128,512]{1,0:T(8,128)(2,1)S(1)} %reshape.135), channel_id=1, source_target_pairs={{0,64},{64,128},{128,192},{192,256},{256,320},{320,384},{384,448},... | collective-permute-start | bytes 393224 | tf_op jit(solution)/shard_map/ppermute | solution.py:39
  33.6 4.5 %collective-permute-start.1 = (bf16[128,512]{1,0:T(8,128)(2,1)S(1)}, bf16[128,512]{1,0:T(8,128)(2,1)S(1)}, u32[]{:S(2)}, u32[]{:S(2)}) collective-permute-start(bf16[128,512]{1,0:T(8,128)(2,1)S(1)} %reshape.135), channel_id=1, source_target_pairs={{0,128},{64,192},{128,256},{192,320},{256,384},{320,448},{384,0},{... | collective-permute-start | bytes 393224 | tf_op jit(solution)/shard_map/ppermute | solution.py:39
  38.2 4.9 %collective-permute-start.2 = (bf16[128,512]{1,0:T(8,128)(2,1)S(1)}, bf16[128,512]{1,0:T(8,128)(2,1)S(1)}, u32[]{:S(2)}, u32[]{:S(2)}) collective-permute-start(bf16[128,512]{1,0:T(8,128)(2,1)S(1)} %reshape.135), channel_id=1, source_target_pairs={{0,192},{64,256},{128,320},{192,384},{256,448},{320,0},{384,64},{4... | collective-permute-start | bytes 393224 | tf_op jit(solution)/shard_map/ppermute | solution.py:39
  43.1 3.8 %collective-permute-start.3 = (bf16[128,512]{1,0:T(8,128)(2,1)S(1)}, bf16[128,512]{1,0:T(8,128)(2,1)S(1)}, u32[]{:S(2)}, u32[]{:S(2)}) collective-permute-start(bf16[128,512]{1,0:T(8,128)(2,1)S(1)} %reshape.135), channel_id=1, source_target_pairs={{0,256},{64,320},{128,384},{192,448},{256,0},{320,64},{384,128},{4... | collective-permute-start | bytes 393224 | tf_op jit(solution)/shard_map/ppermute | solution.py:39
  46.9 5.2 %collective-permute-start.4 = (bf16[128,512]{1,0:T(8,128)(2,1)S(1)}, bf16[128,512]{1,0:T(8,128)(2,1)S(1)}, u32[]{:S(2)}, u32[]{:S(2)}) collective-permute-start(bf16[128,512]{1,0:T(8,128)(2,1)S(1)} %reshape.135), channel_id=1, source_target_pairs={{0,320},{64,384},{128,448},{192,0},{256,64},{320,128},{384,192},{4... | collective-permute-start | bytes 393224 | tf_op jit(solution)/shard_map/ppermute | solution.py:39
  52.1 5.3 %collective-permute-start.5 = (bf16[128,512]{1,0:T(8,128)(2,1)S(1)}, bf16[128,512]{1,0:T(8,128)(2,1)S(1)}, u32[]{:S(2)}, u32[]{:S(2)}) collective-permute-start(bf16[128,512]{1,0:T(8,128)(2,1)S(1)} %reshape.135), channel_id=1, source_target_pairs={{0,384},{64,448},{128,0},{192,64},{256,128},{320,192},{384,256},{4... | collective-permute-start | bytes 393224 | tf_op jit(solution)/shard_map/ppermute | solution.py:39
  57.4 3.3 %collective-permute-start.6 = (bf16[128,512]{1,0:T(8,128)(2,1)S(1)}, bf16[128,512]{1,0:T(8,128)(2,1)S(1)}, u32[]{:S(2)}, u32[]{:S(2)}) collective-permute-start(bf16[128,512]{1,0:T(8,128)(2,1)S(1)} %reshape.135), channel_id=1, source_target_pairs={{0,448},{64,0},{128,64},{192,128},{256,192},{320,256},{384,320},{4... | collective-permute-start | bytes 393224 | tf_op jit(solution)/shard_map/ppermute | solution.py:39
  60.7 5.0 %collective-permute-done.4 = bf16[128,512]{1,0:T(8,128)(2,1)S(1)} collective-permute-done((bf16[128,512]{1,0:T(8,128)(2,1)S(1)}, bf16[128,512]{1,0:T(8,128)(2,1)S(1)}, u32[]{:S(2)}, u32[]{:S(2)}) %collective-permute-start.4) | collective-permute-done | bytes 131104 | tf_op jit(solution)/shard_map/ppermute | solution.py:39
  65.7 3.0 %collective-permute-done.5 = bf16[128,512]{1,0:T(8,128)(2,1)S(1)} collective-permute-done((bf16[128,512]{1,0:T(8,128)(2,1)S(1)}, bf16[128,512]{1,0:T(8,128)(2,1)S(1)}, u32[]{:S(2)}, u32[]{:S(2)}) %collective-permute-start.5) | collective-permute-done | bytes 131104 | tf_op jit(solution)/shard_map/ppermute | solution.py:39
  68.7 1.9 %collective-permute-done.6 = bf16[128,512]{1,0:T(8,128)(2,1)S(1)} collective-permute-done((bf16[128,512]{1,0:T(8,128)(2,1)S(1)}, bf16[128,512]{1,0:T(8,128)(2,1)S(1)}, u32[]{:S(2)}, u32[]{:S(2)}) %collective-permute-start.6) | collective-permute-done | bytes 131104 | tf_op jit(solution)/shard_map/ppermute | solution.py:39
  70.7 1.9 %collective-permute-start.7 = (bf16[1024,512]{1,0:T(8,128)(2,1)S(1)}, bf16[1024,512]{1,0:T(8,128)(2,1)}, u32[]{:S(2)}, u32[]{:S(2)}) collective-permute-start(bf16[1024,512]{1,0:T(8,128)(2,1)S(1)} %constant_dynamic-update-slice_fusion.own_ref), channel_id=1, source_target_pairs={{0,32},{32,0},{1,33},{33,1},{2,34},{34,2},{3,35},{35,3},{4,36},{36... | collective-permute-start | bytes 3145736 | tf_op jit(solution)/shard_map/ppermute | solution.py:43
  73.0 0.3 fusion
  73.4 0.5 copy-done.9
  74.1 1.2 collective-permute-done.7.other_ref
  75.4 2.2 %project.1 = (bf16[128,512]{1,0:T(8,128)(2,1)S(1)}, bf16[128,1024]{1,0:T(8,128)(2,1)S(1)}, bf16[128,1024]{1,0:T(8,128)(2,1)S(1)}) custom-call(s32[2]{0:T(128)S(1)} %pad_add_fusion.place_ref, bf16[256,3584]{1,0:T(8,128)(2,1)S(1)} %bitcast.22, bf16[1024,512]{1,0:T(8,128)(2,1)S(1)} %constant_dynamic-update-slice_fusion.own_ref, ...), custom_call_target="tpu_custom_call" | custom-call | tf_op jit(solution)/shard_map/project/pallas_call | solution.py:348
  77.6 3.4 %collective-permute-start.8 = (bf16[128,512]{1,0:T(8,128)(2,1)S(1)}, bf16[128,512]{1,0:T(8,128)(2,1)S(1)}, u32[]{:S(2)}, u32[]{:S(2)}) collective-permute-start(bf16[128,512]{1,0:T(8,128)(2,1)S(1)} %get-tuple-element.18.k0_ref), channel_id=1, source_target_pairs={{0,1},{1,2},{2,3},{3,4},{4,5},{5,6},{6,7},{7,8},{8,9},{9,10},{10,1... | collective-permute-start | bytes 393224 | tf_op jit(solution)/shard_map/ppermute | solution.py:34
  81.0 4.0 %collective-permute-start.9 = (bf16[128,512]{1,0:T(8,128)(2,1)S(1)}, bf16[128,512]{1,0:T(8,128)(2,1)S(1)}, u32[]{:S(2)}, u32[]{:S(2)}) collective-permute-start(bf16[128,512]{1,0:T(8,128)(2,1)S(1)} %get-tuple-element.18.k0_ref), channel_id=1, source_target_pairs={{0,2},{1,3},{2,4},{3,5},{4,6},{5,7},{6,8},{7,9},{8,10},{9,11},{10,... | collective-permute-start | bytes 393224 | tf_op jit(solution)/shard_map/ppermute | solution.py:34
  85.0 0.6 unpack_rest.1
  85.6 4.9 %collective-permute-done.9.k2_ref = bf16[128,512]{1,0:T(8,128)(2,1)S(1)} collective-permute-done((bf16[128,512]{1,0:T(8,128)(2,1)S(1)}, bf16[128,512]{1,0:T(8,128)(2,1)S(1)}, u32[]{:S(2)}, u32[]{:S(2)}) %collective-permute-start.9) | collective-permute-done | bytes 131104 | tf_op jit(solution)/shard_map/ppermute | solution.py:34
  90.5 4.8 %attend.1 = (f32[128,512]{1,0:T(8,128)S(1)}, bf16[128,512]{1,0:T(8,128)(2,1)S(1)}, bf16[128,512]{1,0:T(8,128)(2,1)S(1)}, f32[1,128]{1,0:T(1,128)}, bf16[4,384,512]{2,1,0:T(8,128)(2,1)S(1)}) custom-call(s32[1,128]{1,0:T(1,128)S(1)} %subtract_bitcast_fusion.start_ref, bf16[128,2048]{1,0:T(8,128)(2,1)S(1)} %get-tuple-element.17.q_ref, ...), custom_call_target="tpu_custom_call" | custom-call | tf_op jit(solution)/shard_map/attend/pallas_call | solution.py:297
  95.3 3.1 %collective-permute-start.11 = (bf16[128,512]{1,0:T(8,128)(2,1)S(1)}, bf16[128,512]{1,0:T(8,128)(2,1)S(1)}, u32[]{:S(2)}, u32[]{:S(2)}) collective-permute-start(bf16[128,512]{1,0:T(8,128)(2,1)S(1)} %get-tuple-element.26), channel_id=1, source_target_pairs={{2,0},{3,1},{4,2},{5,3},{6,4},{7,5},{8,6},{9,7},{10,8},{11,9},{12,... | collective-permute-start | bytes 393224 | tf_op jit(solution)/shard_map/ppermute | solution.py:34
  98.4 3.1 %collective-permute-start.10 = (bf16[128,512]{1,0:T(8,128)(2,1)S(1)}, bf16[128,512]{1,0:T(8,128)(2,1)S(1)}, u32[]{:S(2)}, u32[]{:S(2)}) collective-permute-start(bf16[128,512]{1,0:T(8,128)(2,1)S(1)} %get-tuple-element.25), channel_id=1, source_target_pairs={{1,0},{2,1},{3,2},{4,3},{5,4},{6,5},{7,6},{8,7},{9,8},{10,9},{11,1... | collective-permute-start | bytes 393224 | tf_op jit(solution)/shard_map/ppermute | solution.py:34
  101.5 1.9 %collective-permute-start.12 = (bf16[128,1024]{1,0:T(8,128)(2,1)S(1)}, bf16[128,1024]{1,0:T(8,128)(2,1)S(1)}, u32[]{:S(2)}, u32[]{:S(2)}) collective-permute-start(bf16[128,1024]{1,0:T(8,128)(2,1)S(1)} %get-tuple-element.27), channel_id=1, source_target_pairs={{0,32},{32,0},{1,33},{33,1},{2,34},{34,2},{3,35},{35,3},{4,36},{36... | collective-permute-start | bytes 786440 | tf_op jit(solution)/shard_map/ppermute | solution.py:43
  103.4 1.7 %collective-permute-done.11 = bf16[128,512]{1,0:T(8,128)(2,1)S(1)} collective-permute-done((bf16[128,512]{1,0:T(8,128)(2,1)S(1)}, bf16[128,512]{1,0:T(8,128)(2,1)S(1)}, u32[]{:S(2)}, u32[]{:S(2)}) %collective-permute-start.11) | collective-permute-done | bytes 131104 | tf_op jit(solution)/shard_map/ppermute | solution.py:34
  105.1 0.8 collective-permute-done.10
  106.1 0.3 subtract_convert_fusion
  106.6 1.9 %collective-permute-start.13 = (bf16[128,512]{1,0:T(8,128)(2,1)S(1)}, bf16[128,512]{1,0:T(8,128)(2,1)S(1)}, u32[]{:S(2)}, u32[]{:S(2)}) collective-permute-start(bf16[128,512]{1,0:T(8,128)(2,1)S(1)} %bitcast.30), channel_id=1, source_target_pairs={{0,32},{32,0},{1,33},{33,1},{2,34},{34,2},{3,35},{35,3},{4,36},{36... | collective-permute-start | bytes 393224 | tf_op jit(solution)/shard_map/ppermute | solution.py:43
  108.5 1.3 collective-permute-done.13
  109.8 0.5 fusion.2
  110.3 0.5 add_convert_fusion
  110.8 20.0 %all_to_all.20 = bf16[4,256,512]{2,1,0:T(8,128)(2,1)S(1)} all-to-all(bf16[4,256,512]{2,1,0:T(8,128)(2,1)S(1)} %bitcast.27), channel_id=1, replica_groups=mesh['y'=8,'core'=2,'z'=8,'xh'=2,'xl'=2] {'xh','xl'}, dimensions={0} | all-to-all | bytes 2097152 | tf_op jit(solution)/shard_map/all_to_all | solution.py:28
  131.1 0.8 reshape.140
  131.8 11.1 %all-to-all-start.3 = ((bf16[64,4,512]{2,1,0:T(4,128)(2,1)}), bf16[64,4,512]{2,1,0:T(4,128)(2,1)S(1)}, u32[]{:S(2)}, u32[]{:S(2)}) async-start(bf16[64,4,512]{2,1,0:T(4,128)(2,1)} %reshape.140), calls=%async_computation.3 | async-start | bytes 524288 | tf_op jit(solution)/shard_map/all_to_all | solution.py:28
  142.9 2.1 %collective-permute-start.14 = (bf16[128,512]{1,0:T(8,128)(2,1)S(1)}, bf16[128,512]{1,0:T(8,128)(2,1)S(1)}, u32[]{:S(2)}, u32[]{:S(2)}) collective-permute-start(bf16[128,512]{1,0:T(8,128)(2,1)S(1)} %get-tuple-element.28.v0_ref), channel_id=1, source_target_pairs={{0,1},{1,2},{2,3},{3,4},{4,5},{5,6},{6,7},{7,8},{8,9},{9,10},{10,1... | collective-permute-start | bytes 393224 | tf_op jit(solution)/shard_map/ppermute | solution.py:34
  145.1 6.1 %collective-permute-start.15 = (bf16[128,512]{1,0:T(8,128)(2,1)S(1)}, bf16[128,512]{1,0:T(8,128)(2,1)S(1)}, u32[]{:S(2)}, u32[]{:S(2)}) collective-permute-start(bf16[128,512]{1,0:T(8,128)(2,1)S(1)} %get-tuple-element.28.v0_ref), channel_id=1, source_target_pairs={{0,2},{1,3},{2,4},{3,5},{4,6},{5,7},{6,8},{7,9},{8,10},{9,11},{10,... | collective-permute-start | bytes 393224 | tf_op jit(solution)/shard_map/ppermute | solution.py:34
  151.2 6.3 %collective-permute-done.15.v2_ref = bf16[128,512]{1,0:T(8,128)(2,1)S(1)} collective-permute-done((bf16[128,512]{1,0:T(8,128)(2,1)S(1)}, bf16[128,512]{1,0:T(8,128)(2,1)S(1)}, u32[]{:S(2)}, u32[]{:S(2)}) %collective-permute-start.15) | collective-permute-done | bytes 131104 | tf_op jit(solution)/shard_map/ppermute | solution.py:34
  157.5 1.4 attend_output.1
  158.9 0.6 broadcast_multiply_fusion
  (53 shorter events, 1.6 us)
Async XLA Ops:
  2.0 21.3 %all-to-all-start.1 = ((bf16[32,4,512]{2,1,0:T(4,128)(2,1)}), bf16[32,4,512]{2,1,0:T(4,128)(2,1)S(1)}, u32[]{:S(2)}, u32[]{:S(2)}) async-start(bf16[32,4,512]{2,1,0:T(4,128)(2,1)} %broadcast_in_dim.26), calls=%async_computation.1 | async-start | bytes 262144 | tf_op jit(solution)/shard_map/all_to_all | solution.py:28
  14.6 1.0 copy-start.1
  15.6 1.0 copy-start.2
  16.7 0.9 copy-start.3
  17.6 0.7 copy-start.6
  19.0 1.3 copy-start
  23.3 52.0 %all-to-all-start = ((bf16[32,8,3584]{2,1,0:T(8,128)(2,1)}), bf16[32,8,3584]{2,1,0:T(8,128)(2,1)S(1)}, u32[]{:S(2)}, u32[]{:S(2)}) async-start(bf16[32,8,3584]{2,1,0:T(8,128)(2,1)} %bitcast.24), calls=%async_computation | async-start | bytes 3670016 | tf_op jit(solution)/shard_map/all_to_all | solution.py:28
  30.1 42.5 %copy-start.11 = (s32[1,64]{1,0:T(1,128)S(1)}, s32[1,64]{1,0:T(1,128)}, u32[]{:S(2)}) copy-start(s32[1,64]{1,0:T(1,128)} %param.13) | copy-start | bytes 772
  30.2 21.9 %collective-permute-start = (bf16[128,512]{1,0:T(8,128)(2,1)S(1)}, bf16[128,512]{1,0:T(8,128)(2,1)S(1)}, u32[]{:S(2)}, u32[]{:S(2)}) collective-permute-start(bf16[128,512]{1,0:T(8,128)(2,1)S(1)} %reshape.135), channel_id=1, source_target_pairs={{0,64},{64,128},{128,192},{192,256},{256,320},{320,384},{384,448},... | collective-permute-start | bytes 393224 | tf_op jit(solution)/shard_map/ppermute | solution.py:39
  33.6 23.7 %collective-permute-start.1 = (bf16[128,512]{1,0:T(8,128)(2,1)S(1)}, bf16[128,512]{1,0:T(8,128)(2,1)S(1)}, u32[]{:S(2)}, u32[]{:S(2)}) collective-permute-start(bf16[128,512]{1,0:T(8,128)(2,1)S(1)} %reshape.135), channel_id=1, source_target_pairs={{0,128},{64,192},{128,256},{192,320},{256,384},{320,448},{384,0},{... | collective-permute-start | bytes 393224 | tf_op jit(solution)/shard_map/ppermute | solution.py:39
  38.2 22.5 %collective-permute-start.2 = (bf16[128,512]{1,0:T(8,128)(2,1)S(1)}, bf16[128,512]{1,0:T(8,128)(2,1)S(1)}, u32[]{:S(2)}, u32[]{:S(2)}) collective-permute-start(bf16[128,512]{1,0:T(8,128)(2,1)S(1)} %reshape.135), channel_id=1, source_target_pairs={{0,192},{64,256},{128,320},{192,384},{256,448},{320,0},{384,64},{4... | collective-permute-start | bytes 393224 | tf_op jit(solution)/shard_map/ppermute | solution.py:39
  43.1 17.6 %collective-permute-start.3 = (bf16[128,512]{1,0:T(8,128)(2,1)S(1)}, bf16[128,512]{1,0:T(8,128)(2,1)S(1)}, u32[]{:S(2)}, u32[]{:S(2)}) collective-permute-start(bf16[128,512]{1,0:T(8,128)(2,1)S(1)} %reshape.135), channel_id=1, source_target_pairs={{0,256},{64,320},{128,384},{192,448},{256,0},{320,64},{384,128},{4... | collective-permute-start | bytes 393224 | tf_op jit(solution)/shard_map/ppermute | solution.py:39
  46.9 18.8 %collective-permute-start.4 = (bf16[128,512]{1,0:T(8,128)(2,1)S(1)}, bf16[128,512]{1,0:T(8,128)(2,1)S(1)}, u32[]{:S(2)}, u32[]{:S(2)}) collective-permute-start(bf16[128,512]{1,0:T(8,128)(2,1)S(1)} %reshape.135), channel_id=1, source_target_pairs={{0,320},{64,384},{128,448},{192,0},{256,64},{320,128},{384,192},{4... | collective-permute-start | bytes 393224 | tf_op jit(solution)/shard_map/ppermute | solution.py:39
  52.1 16.6 %collective-permute-start.5 = (bf16[128,512]{1,0:T(8,128)(2,1)S(1)}, bf16[128,512]{1,0:T(8,128)(2,1)S(1)}, u32[]{:S(2)}, u32[]{:S(2)}) collective-permute-start(bf16[128,512]{1,0:T(8,128)(2,1)S(1)} %reshape.135), channel_id=1, source_target_pairs={{0,384},{64,448},{128,0},{192,64},{256,128},{320,192},{384,256},{4... | collective-permute-start | bytes 393224 | tf_op jit(solution)/shard_map/ppermute | solution.py:39
  57.4 13.3 %collective-permute-start.6 = (bf16[128,512]{1,0:T(8,128)(2,1)S(1)}, bf16[128,512]{1,0:T(8,128)(2,1)S(1)}, u32[]{:S(2)}, u32[]{:S(2)}) collective-permute-start(bf16[128,512]{1,0:T(8,128)(2,1)S(1)} %reshape.135), channel_id=1, source_target_pairs={{0,448},{64,0},{128,64},{192,128},{256,192},{320,256},{384,320},{4... | collective-permute-start | bytes 393224 | tf_op jit(solution)/shard_map/ppermute | solution.py:39
  70.7 4.7 %collective-permute-start.7 = (bf16[1024,512]{1,0:T(8,128)(2,1)S(1)}, bf16[1024,512]{1,0:T(8,128)(2,1)}, u32[]{:S(2)}, u32[]{:S(2)}) collective-permute-start(bf16[1024,512]{1,0:T(8,128)(2,1)S(1)} %constant_dynamic-update-slice_fusion.own_ref), channel_id=1, source_target_pairs={{0,32},{32,0},{1,33},{33,1},{2,34},{34,2},{3,35},{35,3},{4,36},{36... | collective-permute-start | bytes 3145736 | tf_op jit(solution)/shard_map/ppermute | solution.py:43
  73.3 0.6 copy-start.9
  73.3 2.0 %copy-start.7 = (f32[128,64]{1,0:T(8,128)}, f32[128,64]{1,0:T(8,128)S(1)}, u32[]{:S(2)}) copy-start(f32[128,64]{1,0:T(8,128)S(1)} %get-tuple-element.33) | copy-start | bytes 98308
  75.3 15.2 %copy-start.4 = (s32[128,128]{1,0:T(8,128)S(1)}, s32[128,128]{1,0:T(8,128)}, u32[]{:S(2)}) copy-start(s32[128,128]{1,0:T(8,128)} %pick_ref.1) | copy-start | bytes 196612
  75.3 15.2 %copy-start.5 = (f32[128,128]{1,0:T(8,128)S(1)}, f32[128,128]{1,0:T(8,128)}, u32[]{:S(2)}) copy-start(f32[128,128]{1,0:T(8,128)} %prob_ref.1) | copy-start | bytes 196612
  77.6 8.0 %collective-permute-start.8 = (bf16[128,512]{1,0:T(8,128)(2,1)S(1)}, bf16[128,512]{1,0:T(8,128)(2,1)S(1)}, u32[]{:S(2)}, u32[]{:S(2)}) collective-permute-start(bf16[128,512]{1,0:T(8,128)(2,1)S(1)} %get-tuple-element.18.k0_ref), channel_id=1, source_target_pairs={{0,1},{1,2},{2,3},{3,4},{4,5},{5,6},{6,7},{7,8},{8,9},{9,10},{10,1... | collective-permute-start | bytes 393224 | tf_op jit(solution)/shard_map/ppermute | solution.py:34
  81.0 9.6 %collective-permute-start.9 = (bf16[128,512]{1,0:T(8,128)(2,1)S(1)}, bf16[128,512]{1,0:T(8,128)(2,1)S(1)}, u32[]{:S(2)}, u32[]{:S(2)}) collective-permute-start(bf16[128,512]{1,0:T(8,128)(2,1)S(1)} %get-tuple-element.18.k0_ref), channel_id=1, source_target_pairs={{0,2},{1,3},{2,4},{3,5},{4,6},{5,7},{6,8},{7,9},{8,10},{9,11},{10,... | collective-permute-start | bytes 393224 | tf_op jit(solution)/shard_map/ppermute | solution.py:34
  85.0 21.1 %copy-start.8 = (f32[128,64]{1,0:T(8,128)S(1)}, f32[128,64]{1,0:T(8,128)}, u32[]{:S(2)}) copy-start(f32[128,64]{1,0:T(8,128)} %copy-done.7) | copy-start | bytes 98308
  85.0 21.1 %copy-start.10 = (f32[128,64]{1,0:T(8,128)S(1)}, f32[128,64]{1,0:T(8,128)}, u32[]{:S(2)}) copy-start(f32[128,64]{1,0:T(8,128)} %copy-done.9) | copy-start | bytes 98308
  95.3 9.8 %collective-permute-start.11 = (bf16[128,512]{1,0:T(8,128)(2,1)S(1)}, bf16[128,512]{1,0:T(8,128)(2,1)S(1)}, u32[]{:S(2)}, u32[]{:S(2)}) collective-permute-start(bf16[128,512]{1,0:T(8,128)(2,1)S(1)} %get-tuple-element.26), channel_id=1, source_target_pairs={{2,0},{3,1},{4,2},{5,3},{6,4},{7,5},{8,6},{9,7},{10,8},{11,9},{12,... | collective-permute-start | bytes 393224 | tf_op jit(solution)/shard_map/ppermute | solution.py:34
  98.4 7.5 %collective-permute-start.10 = (bf16[128,512]{1,0:T(8,128)(2,1)S(1)}, bf16[128,512]{1,0:T(8,128)(2,1)S(1)}, u32[]{:S(2)}, u32[]{:S(2)}) collective-permute-start(bf16[128,512]{1,0:T(8,128)(2,1)S(1)} %get-tuple-element.25), channel_id=1, source_target_pairs={{1,0},{2,1},{3,2},{4,3},{5,4},{6,5},{7,6},{8,7},{9,8},{10,9},{11,1... | collective-permute-start | bytes 393224 | tf_op jit(solution)/shard_map/ppermute | solution.py:34
  101.5 7.0 %collective-permute-start.12 = (bf16[128,1024]{1,0:T(8,128)(2,1)S(1)}, bf16[128,1024]{1,0:T(8,128)(2,1)S(1)}, u32[]{:S(2)}, u32[]{:S(2)}) collective-permute-start(bf16[128,1024]{1,0:T(8,128)(2,1)S(1)} %get-tuple-element.27), channel_id=1, source_target_pairs={{0,32},{32,0},{1,33},{33,1},{2,34},{34,2},{3,35},{35,3},{4,36},{36... | collective-permute-start | bytes 786440 | tf_op jit(solution)/shard_map/ppermute | solution.py:43
  106.6 3.2 %collective-permute-start.13 = (bf16[128,512]{1,0:T(8,128)(2,1)S(1)}, bf16[128,512]{1,0:T(8,128)(2,1)S(1)}, u32[]{:S(2)}, u32[]{:S(2)}) collective-permute-start(bf16[128,512]{1,0:T(8,128)(2,1)S(1)} %bitcast.30), channel_id=1, source_target_pairs={{0,32},{32,0},{1,33},{33,1},{2,34},{34,2},{3,35},{35,3},{4,36},{36... | collective-permute-start | bytes 393224 | tf_op jit(solution)/shard_map/ppermute | solution.py:43
  131.8 27.0 %all-to-all-start.3 = ((bf16[64,4,512]{2,1,0:T(4,128)(2,1)}), bf16[64,4,512]{2,1,0:T(4,128)(2,1)S(1)}, u32[]{:S(2)}, u32[]{:S(2)}) async-start(bf16[64,4,512]{2,1,0:T(4,128)(2,1)} %reshape.140), calls=%async_computation.3 | async-start | bytes 524288 | tf_op jit(solution)/shard_map/all_to_all | solution.py:28
  142.9 8.3 %collective-permute-start.14 = (bf16[128,512]{1,0:T(8,128)(2,1)S(1)}, bf16[128,512]{1,0:T(8,128)(2,1)S(1)}, u32[]{:S(2)}, u32[]{:S(2)}) collective-permute-start(bf16[128,512]{1,0:T(8,128)(2,1)S(1)} %get-tuple-element.28.v0_ref), channel_id=1, source_target_pairs={{0,1},{1,2},{2,3},{3,4},{4,5},{5,6},{6,7},{7,8},{8,9},{9,10},{10,1... | collective-permute-start | bytes 393224 | tf_op jit(solution)/shard_map/ppermute | solution.py:34
  145.1 12.4 %collective-permute-start.15 = (bf16[128,512]{1,0:T(8,128)(2,1)S(1)}, bf16[128,512]{1,0:T(8,128)(2,1)S(1)}, u32[]{:S(2)}, u32[]{:S(2)}) collective-permute-start(bf16[128,512]{1,0:T(8,128)(2,1)S(1)} %get-tuple-element.28.v0_ref), channel_id=1, source_target_pairs={{0,2},{1,3},{2,4},{3,5},{4,6},{5,7},{6,8},{7,9},{8,10},{9,11},{10,... | collective-permute-start | bytes 393224 | tf_op jit(solution)/shard_map/ppermute | solution.py:34
